TPU v7x, 256 devices: a whole 4x4x8 slice. The times are simulated.
256 devices in a mesh: rep: 4 (over y), tp: 64 (over x, z, core).
Axes of the slice: x: 4, y: 4, z: 8, core: 2. Of those that a mesh axis runs over, the one named last changes fastest.
Arguments:
- stream: bfloat16 [1024, 5120], P(('rep', 'tp')), parts along dimension 0, may hold values from -6 to 6
- attn_gain: bfloat16 [5120], replicated, may hold values from 0.5 to 1.5
- query_weight: bfloat16 [5120, 64, 80], P(None, 'tp'), may hold values from -0.078125 to 0.078125
- query_bias_input: bfloat16 [64, 80], P('tp'), may hold values from -2 to 18
- key_value_weight: bfloat16 [5120, 64, 32], P(None, 'tp'), may hold values from -0.078125 to 0.078125
- key_value_bias: bfloat16 [64, 32], P('tp'), may hold values from -2 to 16
- output_weight: bfloat16 [64, 80, 5120], P('tp'), may hold values from -0.078125 to 0.078125
- mlp_gain: bfloat16 [5120], replicated, may hold values from 0.5 to 1.5
- w_gate: bfloat16 [5120, 16384], P(None, 'tp'), may hold values from -0.078125 to 0.078125
- w_up: bfloat16 [5120, 16384], P(None, 'tp'), may hold values from -0.078125 to 0.078125
- w_down: bfloat16 [16384, 5120], P('tp'), may hold values from -0.046875 to 0.046875
- paged_cache_input: bfloat16 [256, 64, 16, 256], P(('rep', 'tp')), parts along dimension 0, may hold values from -6 to 6
- lengths: int32 [8], P('rep'), parts along dimension 0, may hold values from 768 to 3072, as said below
- page_table: int32 [8, 192], P('rep'), parts along dimension 0, may hold values from 0 to 511, as said below
- new_pages: int32 [8, 8], P('rep'), parts along dimension 0, may hold values from 0 to 511, as said below
- mig_from: int32 [32, 8], P('rep'), parts along dimension 0, may hold values from 0 to 63, as said below
- mig_to: int32 [32, 8], P('rep'), parts along dimension 0, may hold values from 0 to 63, as said below
Outputs:
- layer_out: bfloat16 [1024, 5120], P(('rep', 'tp')), parts along dimension 0
- updated_cache: bfloat16 [256, 64, 16, 256], P(('rep', 'tp')), parts along dimension 0
There are 4 independent parts, one for each index of `rep`. A program takes and returns all parts, laid end to end along the dimension named above; an argument that names none is the same for every part. Nothing has to cross between parts.
Inputs may be any that keep to these rules, and one draw needn't show every extreme that they name: `lengths`: one prompt holds exactly 3072 cached tokens. Entries of page_table and new_pages are all distinct; entries past a prompt's length are not read. `new_pages`: distinct from every page_table entry. `mig_from`: 8 distinct slots of owner b that no table names. `mig_to`: 8 distinct slots of owner (b + 1) mod 8, each named by page_table within its prompt's length.
All inputs are finite; a program needn't handle non-finite values.
Results may differ from a plain program's by a relative error of at most 0.0085.
The roundings to bfloat16 on the way count: a program that leaves them out, or rounds other values in their place, can miss the bound.
Values may be sent and summed in bfloat16 or wider, within the bound.
A program may use at most 128 MiB of HBM per device.

v0:
```python
import jax
import jax.numpy as jnp
from jax import lax
from jax.sharding import PartitionSpec as P

KEY_VALUE_HEADS = 8
HEAD_SIZE = 128
BATCH_REQUESTS = 2
SPAN = 128
PROMPTS = 2
PAGE_TOKENS = 16
QUERY_PER_KV = 5
MAXP = 192
REQUEST_PAGES = 8
NEW_TOKEN_COUNT = 256


EPSILON = 1e-06
ROPE_BASE = 1000000.0
NEG_LARGE = -1e30


def from_partner(value, axis, distance):
    mask = 2**distance
    pairs = [(source, source ^ mask) for source in range(lax.axis_size(axis))]
    return lax.ppermute(value, axis, pairs)


def passed_along(value, axis, steps):
    count = lax.axis_size(axis)
    pairs = [(source, (source + steps) % count) for source in range(count)]
    return lax.ppermute(value, axis, pairs)


def rms_scale(values, gain_vec):
    widened = values.astype(jnp.float32)
    spread = jnp.mean(widened * widened, axis=-1, keepdims=True)
    return (widened * lax.rsqrt(spread + EPSILON) * gain_vec.astype(jnp.float32)).astype(
        jnp.bfloat16
    )


def rotary(values, positions):
    half_dim = values.shape[-1] // 2
    frequencies = ROPE_BASE ** (-(2.0 * jnp.arange(half_dim, dtype=jnp.float32)) / values.shape[-1])
    angles = positions.astype(jnp.float32)[:, None] * frequencies[None, :]
    cosine = jnp.cos(angles)[:, None, :]
    sine_part = jnp.sin(angles)[:, None, :]
    first_half = values[..., :half_dim]
    second = values[..., half_dim:]
    return jnp.concatenate(
        [first_half * cosine - second * sine_part, second * cosine + first_half * sine_part],
        axis=-1,
    )


def token_info(lengths):
    token_ids = jnp.arange(NEW_TOKEN_COUNT, dtype=jnp.int32)
    request_of = token_ids // SPAN
    offset_of = token_ids % SPAN
    positions = jnp.take(lengths, request_of) + offset_of
    return (request_of, offset_of, request_of, positions)


def slot_roles(slot_ids, page_table, new_pages):
    old_hit = (page_table[:, :, None] == slot_ids[None, None, :]).astype(jnp.int32)
    old_valid = jnp.sum(old_hit, axis=(0, 1))
    old_prompt = jnp.sum(old_hit * jnp.arange(PROMPTS, dtype=jnp.int32)[:, None, None], axis=(0, 1))
    old_page = jnp.sum(old_hit * jnp.arange(MAXP, dtype=jnp.int32)[None, :, None], axis=(0, 1))
    new_hit = (new_pages[:, :, None] == slot_ids[None, None, :]).astype(jnp.int32)
    new_valid = jnp.sum(new_hit, axis=(0, 1))
    new_request = jnp.sum(
        new_hit * jnp.arange(BATCH_REQUESTS, dtype=jnp.int32)[:, None, None], axis=(0, 1)
    )
    new_page = jnp.sum(
        new_hit * jnp.arange(REQUEST_PAGES, dtype=jnp.int32)[None, :, None], axis=(0, 1)
    )
    return (old_valid, old_prompt, old_page, new_valid, new_request, new_page)


def key_allowed(roles, lengths, request_of, offset_of, prompt_of):
    old_valid, old_prompt, old_page, new_valid, new_request, new_page = roles
    within_page = jnp.arange(PAGE_TOKENS, dtype=jnp.int32)
    old_pos = (old_page[:, None] * PAGE_TOKENS + within_page[None, :]).reshape(-1)
    new_pos = (new_page[:, None] * PAGE_TOKENS + within_page[None, :]).reshape(-1)
    old_limit = jnp.repeat(jnp.take(lengths, old_prompt), PAGE_TOKENS)
    old_ok = (
        (jnp.repeat(old_valid, PAGE_TOKENS) == 1)[None, :]
        & (jnp.repeat(old_prompt, PAGE_TOKENS)[None, :] == prompt_of[:, None])
        & (old_pos < old_limit)[None, :]
    )
    new_ok = (
        (jnp.repeat(new_valid, PAGE_TOKENS) == 1)[None, :]
        & (jnp.repeat(new_request, PAGE_TOKENS)[None, :] == request_of[:, None])
        & (new_pos[None, :] <= offset_of[:, None])
    )
    return old_ok | new_ok


def per_device(
    stream,
    attn_gain,
    query_weight,
    query_bias_input,
    key_value_weight,
    key_value_bias,
    output_weight,
    mlp_gain,
    w_gate,
    w_up,
    w_down,
    paged_cache_input,
    lengths,
    page_table,
    new_pages,
    mig_from,
    mig_to,
):
    device_total = lax.axis_size("tp")
    owner_total = device_total // KEY_VALUE_HEADS
    level_count = owner_total.bit_length() - 1
    group_flag = KEY_VALUE_HEADS.bit_length() - 1
    token_position = lax.axis_index("tp")
    owner_index = token_position // KEY_VALUE_HEADS
    tok_rows = stream.shape[0]
    total_rows = tok_rows * device_total
    query_cols = query_weight.shape[2]
    proj_weight = jnp.concatenate([query_weight[:, 0, :], key_value_weight[:, 0, :]], axis=1)
    proj_bias = jnp.concatenate([query_bias_input[0], key_value_bias[0]]).astype(jnp.float32)
    normed = rms_scale(stream, attn_gain)
    projected = (
        jnp.dot(
            lax.all_gather(normed, "tp", axis=0, tiled=True),
            proj_weight,
            preferred_element_type=jnp.float32,
        )
        + proj_bias
    ).astype(jnp.bfloat16)
    gathered = projected
    for each_level in range(level_count):
        partner = from_partner(gathered, "tp", group_flag + each_level)
        upper_side = owner_index >> each_level & 1 == 1
        gathered = jnp.where(
            upper_side,
            jnp.concatenate([partner, gathered], axis=1),
            jnp.concatenate([gathered, partner], axis=1),
        )
    pieces = gathered.reshape(total_rows, owner_total, -1)
    queries = pieces[:, :, :query_cols].reshape(total_rows, QUERY_PER_KV, HEAD_SIZE)
    key_value_rows = pieces[:, :, query_cols:].reshape(total_rows, 2 * HEAD_SIZE)
    request_of, offset_of, prompt_of, positions = token_info(lengths)
    rotated_queries = rotary(queries.astype(jnp.float32), positions).astype(jnp.bfloat16)
    keys_rot = rotary(key_value_rows[:, None, :HEAD_SIZE].astype(jnp.float32), positions)[
        :, 0
    ].astype(jnp.bfloat16)
    appended_rows = jnp.concatenate([keys_rot, key_value_rows[:, HEAD_SIZE:]], axis=1)
    local_cache = paged_cache_input[0]
    slot_count = local_cache.shape[0]
    departing_pages = local_cache[
        lax.dynamic_index_in_dim(mig_from, owner_index, 0, keepdims=False)
    ]
    received_pages = passed_along(departing_pages, "tp", KEY_VALUE_HEADS)
    sender = (owner_index + owner_total - 1) % owner_total
    landing = lax.dynamic_index_in_dim(mig_to, sender, 0, keepdims=False)
    local_cache = local_cache.at[landing].set(received_pages)
    slot_ids = owner_index * slot_count + jnp.arange(slot_count, dtype=jnp.int32)
    roles = slot_roles(slot_ids, page_table, new_pages)
    new_valid, new_request, new_page = (roles[3], roles[4], roles[5])
    source_rows = (new_request * SPAN + new_page * PAGE_TOKENS)[:, None] + jnp.arange(
        PAGE_TOKENS, dtype=jnp.int32
    )[None, :]
    fresh_pages = appended_rows[source_rows]
    local_cache = jnp.where((new_valid == 1)[:, None, None], fresh_pages, local_cache)
    updated_cache = local_cache[None]
    allowed = key_allowed(roles, lengths, request_of, offset_of, prompt_of)
    flat_keys = local_cache.reshape(slot_count * PAGE_TOKENS, 2 * HEAD_SIZE)
    scores = jnp.einsum(
        "tqd,kd->qtk", rotated_queries, flat_keys[:, :HEAD_SIZE], preferred_element_type=jnp.float32
    ) * HEAD_SIZE ** (-0.5)
    live_mask = allowed[None]
    part_max = jnp.max(jnp.where(live_mask, scores, NEG_LARGE), axis=-1)
    weights = jnp.where(live_mask, jnp.exp(scores - part_max[..., None]), 0.0)
    part_sum = jnp.sum(weights, axis=-1).T
    part_max = part_max.T
    prob_bf = weights.astype(jnp.bfloat16)
    part_out = jnp.einsum(
        "qtk,kd->tqd", prob_bf, flat_keys[:, HEAD_SIZE:], preferred_element_type=jnp.float32
    )
    merged = part_out.reshape(total_rows, QUERY_PER_KV * HEAD_SIZE)
    for each_level in range(level_count):
        other_out, other_max, other_sum = from_partner(
            (merged, part_max, part_sum), "tp", group_flag + each_level
        )
        both_max = jnp.maximum(part_max, other_max)
        mine_weight = jnp.exp(part_max - both_max)
        other_weight = jnp.exp(other_max - both_max)
        merged = (
            merged.reshape(total_rows, QUERY_PER_KV, HEAD_SIZE) * mine_weight[..., None]
            + other_out.reshape(total_rows, QUERY_PER_KV, HEAD_SIZE) * other_weight[..., None]
        ).reshape(total_rows, QUERY_PER_KV * HEAD_SIZE)
        part_sum = mine_weight * part_sum + other_weight * other_sum
        part_max = both_max
    normalized = (
        merged.reshape(total_rows, QUERY_PER_KV, HEAD_SIZE) / part_sum[..., None]
    ).reshape(total_rows, QUERY_PER_KV * HEAD_SIZE)
    attn_piece = lax.dynamic_slice_in_dim(
        normalized, owner_index * query_cols, query_cols, 1
    ).astype(jnp.bfloat16)
    out_rows = output_weight[0]
    attn_sum = lax.psum_scatter(
        jnp.dot(attn_piece, out_rows, preferred_element_type=jnp.float32),
        "tp",
        scatter_dimension=0,
        tiled=True,
    )
    mixed_rows = (stream.astype(jnp.float32) + attn_sum).astype(jnp.bfloat16)
    piece = lax.all_gather(rms_scale(mixed_rows, mlp_gain), "tp", axis=0, tiled=True)
    gate_acts = jnp.dot(piece, w_gate, preferred_element_type=jnp.float32)
    up_acts = jnp.dot(piece, w_up, preferred_element_type=jnp.float32)
    hidden = (jax.nn.silu(gate_acts) * up_acts).astype(jnp.bfloat16)
    mlp_sum = lax.psum_scatter(
        jnp.dot(hidden, w_down, preferred_element_type=jnp.float32),
        "tp",
        scatter_dimension=0,
        tiled=True,
    )
    layer_out = (mixed_rows.astype(jnp.float32) + mlp_sum).astype(jnp.bfloat16)
    return (layer_out, updated_cache)


def solution(mesh):
    placed = (
        P(("rep", "tp"), None),
        P(),
        P(None, "tp", None),
        P("tp", None),
        P(None, "tp", None),
        P("tp", None),
        P("tp", None, None),
        P(),
        P(None, "tp"),
        P(None, "tp"),
        P("tp", None),
        P(("rep", "tp"), None, None, None),
        P("rep"),
        P("rep", None),
        P("rep", None),
        P("rep", None),
        P("rep", None),
    )
    return jax.shard_map(
        per_device,
        mesh=mesh,
        in_specs=placed,
        out_specs=(P(("rep", "tp"), None), P(("rep", "tp"), None, None, None)),
        check_vma=False,
    )
```

profile of v0, /device:TPU:16, one launch (start us, length us, event | category | flops | bytes accessed | tf_op | source)
XLA Modules:
  0.0 707.2 jit_solution(9521984146199086762)
XLA Ops:
  10.1 1.5 fusion.54
  13.5 7.2 %collective-permute-start.3 = (bf16[8,16,256]{2,1,0:T(8,128)(2,1)}, bf16[8,16,256]{2,1,0:T(8,128)(2,1)}, u32[]{:S(2)}, u32[]{:S(2)}) collective-permute-start(bf16[8,16,256]{2,1,0:T(8,128)(2,1)} %gather_fusion.1), channel_id=1, source_target_pairs={{0,8},{1,9},{2,10},{3,11},{4,12},{5,13},{6,14},{7,15},{8,16},{9,17... | collective-permute-start | bytes 196616 | tf_op jit(solution)/shard_map/ppermute | solution.py:32
  30.5 61.6 %all-gather.5.cloned.1.call-done = bf16[64,4,5120]{2,1,0:T(4,128)(2,1)} async-done(((bf16[1,4,5120]{2,1,0:T(4,128)(2,1)}), bf16[64,4,5120]{2,1,0:T(4,128)(2,1)}) %all-gather.5.cloned.1.call-update) | async-done | bytes 2621456 | tf_op jit(solution)/shard_map/all_gather | solution.py:133
  92.2 5.2 reshape.651
  97.4 3.0 fusion.17
  100.4 3.3 collective-permute-start
  103.8 4.9 collective-permute-done
  110.8 1.4 scatter_fusion
  112.3 2.3 collective-permute-done.1
  115.7 3.3 collective-permute-start.2
  120.9 2.4 collective-permute-done.2
  124.8 2.1 copy.52
  126.9 2.1 copy.51
  128.9 5.0 gather_fusion
  135.1 1.7 subtract_convert_fusion
  139.2 3.2 collective-permute-start.5
  143.6 2.9 collective-permute-start.10
  146.4 3.2 collective-permute-start.4
  149.6 7.6 %collective-permute-done.10 = f32[256,5]{0,1:T(8,128)S(1)} collective-permute-done((f32[256,5]{0,1:T(8,128)S(1)}, f32[256,5]{0,1:T(8,128)S(1)}, u32[]{:S(2)}, u32[]{:S(2)}) %collective-permute-start.10) | collective-permute-done | bytes 5152 | tf_op jit(solution)/shard_map/ppermute | solution.py:26
  157.9 1.6 collective-permute-start.11
  159.9 10.5 %collective-permute-done.11 = f32[256,5]{0,1:T(8,128)S(1)} collective-permute-done((f32[256,5]{0,1:T(8,128)S(1)}, f32[256,5]{0,1:T(8,128)S(1)}, u32[]{:S(2)}, u32[]{:S(2)}) %collective-permute-start.11) | collective-permute-done | bytes 5152 | tf_op jit(solution)/shard_map/ppermute | solution.py:26
  170.7 10.7 %collective-permute-start.9 = (f32[256,640]{0,1:T(8,128)S(1)}, f32[256,640]{0,1:T(8,128)}, u32[]{:S(2)}, u32[]{:S(2)}) collective-permute-start(f32[256,640]{0,1:T(8,128)S(1)} %bitcast.108), channel_id=1, source_target_pairs={{0,32},{1,33},{2,34},{3,35},{4,36},{5,37},{6,38},{7,39},{8,40},{9,... | collective-permute-start | bytes 1966088 | tf_op jit(solution)/shard_map/ppermute | solution.py:26
  181.4 3.4 collective-permute-start.8
  184.9 6.0 collective-permute-done.12
  192.2 4.4 fusion.20
  198.5 208.4 %all-reduce.5.cloned.1.call-done = f32[256,5120]{1,0:T(8,128)} async-done(((f32[256,5120]{1,0:T(8,128)}), f32[256,5120]{1,0:T(8,128)}) %all-reduce.5.cloned.1.call-update) | async-done | bytes 5242896
  408.8 78.0 %all-gather.7.cloned.1.call-done = bf16[64,4,5120]{2,1,0:T(4,128)(2,1)} async-done(((bf16[1,4,5120]{2,1,0:T(4,128)(2,1)}), bf16[64,4,5120]{2,1,0:T(4,128)(2,1)}) %all-gather.7.cloned.1.call-update) | async-done | bytes 2621456 | tf_op jit(solution)/shard_map/all_gather | solution.py:217
  486.7 5.2 reshape.653
  492.0 3.4 fusion.80
  495.3 7.7 %fusion.9 = f32[256,5120]{1,0:T(8,128)} fusion(bf16[256,5120]{1,0:T(8,128)(2,1)S(1)} %copy-done, bf16[256,5120]{1,0:T(8,128)(2,1)} %reshape.653, bf16[5120,256]{1,0:T(8,128)(2,1)} %param.26, f32[256,256]{1,0:T(8,128)S(1)} %fusion.80), kind=kOutput, calls=%fused_computation.14 | convolution fusion | flops 1342570496 | bytes 13369344 | tf_op jit(solution)/shard_map/dot_general | solution.py:222
  503.1 196.0 %all-reduce.7.cloned.1.call-done = f32[256,5120]{1,0:T(8,128)} async-done(((f32[256,5120]{1,0:T(8,128)}), f32[256,5120]{1,0:T(8,128)}) %all-reduce.7.cloned.1.call-update) | async-done | bytes 5242896
  699.1 1.6 fusion.47
  (101 shorter events, 31.9 us)
Async XLA Ops:
  7.2 488.2 %copy-start = (bf16[256,5120]{1,0:T(8,128)(2,1)S(1)}, bf16[256,5120]{1,0:T(8,128)(2,1)}, u32[]{:S(2)}) copy-start(bf16[256,5120]{1,0:T(8,128)(2,1)} %param.27) | copy-start | bytes 7864324
  7.2 85.0 %all-gather.5.cloned.1.call-start = ((), (), s32[]{:S(2)}) async-start(), calls=%async_computation | async-start | bytes 2662400 | tf_op jit(solution)/shard_map/all_gather | solution.py:133
  11.6 395.3 %all-reduce.5.cloned.1.call-start = ((), (), s32[]{:S(2)}) async-start(), calls=%async_computation.2 | async-start | bytes 10485760
  13.5 97.3 %collective-permute-start.3 = (bf16[8,16,256]{2,1,0:T(8,128)(2,1)}, bf16[8,16,256]{2,1,0:T(8,128)(2,1)}, u32[]{:S(2)}, u32[]{:S(2)}) collective-permute-start(bf16[8,16,256]{2,1,0:T(8,128)(2,1)} %gather_fusion.1), channel_id=1, source_target_pairs={{0,8},{1,9},{2,10},{3,11},{4,12},{5,13},{6,14},{7,15},{8,16},{9,17... | collective-permute-start | bytes 196616 | tf_op jit(solution)/shard_map/ppermute | solution.py:32
  100.4 3.4 copy-start.5
  100.4 8.3 %collective-permute-start = (bf16[256,112]{0,1:T(8,128)(2,1)S(1)}, bf16[256,112]{0,1:T(8,128)(2,1)}, u32[]{:S(2)}, u32[]{:S(2)}) collective-permute-start(bf16[256,112]{0,1:T(8,128)(2,1)S(1)} %fusion.17), channel_id=1, source_target_pairs={{0,8},{1,9},{2,10},{3,11},{4,12},{5,13},{6,14},{7,15},{8,0},{9,1},... | collective-permute-start | bytes 172040 | tf_op jit(solution)/shard_map/ppermute | solution.py:26
  109.6 5.0 collective-permute-start.1
  112.3 11.1 %copy-start.1 = (bf16[64,16,256]{2,1,0:T(8,128)(2,1)}, bf16[64,16,256]{2,1,0:T(8,128)(2,1)S(1)}, u32[]{:S(2)}) copy-start(bf16[64,16,256]{2,1,0:T(8,128)(2,1)S(1)} %scatter_fusion) | copy-start | bytes 1572868
  115.7 7.6 %collective-permute-start.2 = (bf16[256,448]{0,1:T(8,128)(2,1)S(1)}, bf16[256,448]{0,1:T(8,128)(2,1)S(1)}, u32[]{:S(2)}, u32[]{:S(2)}) collective-permute-start(bf16[256,448]{0,1:T(8,128)(2,1)S(1)} %maximum_select_fusion.1), channel_id=1, source_target_pairs={{0,32},{1,33},{2,34},{3,35},{4,36},{5,37},{6,38},{7,39},{8,40},{9,... | collective-permute-start | bytes 688136 | tf_op jit(solution)/shard_map/ppermute | solution.py:26
  128.9 5.0 copy-start.2
  135.1 2.9 copy-start.3
  139.2 18.0 %collective-permute-start.5 = (f32[256,640]{0,1:T(8,128)S(1)}, f32[256,640]{0,1:T(8,128)S(1)}, u32[]{:S(2)}, u32[]{:S(2)}) collective-permute-start(f32[256,640]{0,1:T(8,128)S(1)} %bitcast.114), channel_id=1, source_target_pairs={{0,8},{1,9},{2,10},{3,11},{4,12},{5,13},{6,14},{7,15},{8,0},{9,1},... | collective-permute-start | bytes 1966088 | tf_op jit(solution)/shard_map/ppermute | solution.py:26
  143.6 13.6 %collective-permute-start.10 = (f32[256,5]{0,1:T(8,128)S(1)}, f32[256,5]{0,1:T(8,128)S(1)}, u32[]{:S(2)}, u32[]{:S(2)}) collective-permute-start(f32[256,5]{0,1:T(8,128)S(1)} %bitcast.122), channel_id=1, source_target_pairs={{0,8},{1,9},{2,10},{3,11},{4,12},{5,13},{6,14},{7,15},{8,0},{9,1},... | collective-permute-start | bytes 15368 | tf_op jit(solution)/shard_map/ppermute | solution.py:26
  146.4 10.8 %collective-permute-start.4 = (f32[256,5]{0,1:T(8,128)S(1)}, f32[256,5]{0,1:T(8,128)S(1)}, u32[]{:S(2)}, u32[]{:S(2)}) collective-permute-start(f32[256,5]{0,1:T(8,128)S(1)} %bitcast.121), channel_id=1, source_target_pairs={{0,8},{1,9},{2,10},{3,11},{4,12},{5,13},{6,14},{7,15},{8,0},{9,1},... | collective-permute-start | bytes 15368 | tf_op jit(solution)/shard_map/ppermute | solution.py:26
  157.4 13.2 %collective-permute-start.7 = (f32[256,640]{0,1:T(8,128)S(1)}, f32[256,640]{0,1:T(8,128)S(1)}, u32[]{:S(2)}, u32[]{:S(2)}) collective-permute-start(f32[256,640]{0,1:T(8,128)S(1)} %bitcast.109), channel_id=1, source_target_pairs={{0,16},{1,17},{2,18},{3,19},{4,20},{5,21},{6,22},{7,23},{8,24},{9,... | collective-permute-start | bytes 1966088 | tf_op jit(solution)/shard_map/ppermute | solution.py:26
  157.9 12.6 %collective-permute-start.11 = (f32[256,5]{0,1:T(8,128)S(1)}, f32[256,5]{0,1:T(8,128)S(1)}, u32[]{:S(2)}, u32[]{:S(2)}) collective-permute-start(f32[256,5]{0,1:T(8,128)S(1)} %get-tuple-element.17), channel_id=1, source_target_pairs={{0,16},{1,17},{2,18},{3,19},{4,20},{5,21},{6,22},{7,23},{8,24},{9,... | collective-permute-start | bytes 15368 | tf_op jit(solution)/shard_map/ppermute | solution.py:26
  159.5 11.1 %collective-permute-start.6 = (f32[256,5]{0,1:T(8,128)S(1)}, f32[256,5]{0,1:T(8,128)S(1)}, u32[]{:S(2)}, u32[]{:S(2)}) collective-permute-start(f32[256,5]{0,1:T(8,128)S(1)} %get-tuple-element.20), channel_id=1, source_target_pairs={{0,16},{1,17},{2,18},{3,19},{4,20},{5,21},{6,22},{7,23},{8,24},{9,... | collective-permute-start | bytes 15368 | tf_op jit(solution)/shard_map/ppermute | solution.py:26
  170.7 20.3 %collective-permute-start.9 = (f32[256,640]{0,1:T(8,128)S(1)}, f32[256,640]{0,1:T(8,128)}, u32[]{:S(2)}, u32[]{:S(2)}) collective-permute-start(f32[256,640]{0,1:T(8,128)S(1)} %bitcast.108), channel_id=1, source_target_pairs={{0,32},{1,33},{2,34},{3,35},{4,36},{5,37},{6,38},{7,39},{8,40},{9,... | collective-permute-start | bytes 1966088 | tf_op jit(solution)/shard_map/ppermute | solution.py:26
  181.3 9.5 %collective-permute-start.12 = (f32[256,5]{0,1:T(8,128)S(1)}, f32[256,5]{0,1:T(8,128)S(1)}, u32[]{:S(2)}, u32[]{:S(2)}) collective-permute-start(f32[256,5]{0,1:T(8,128)S(1)} %get-tuple-element.13), channel_id=1, source_target_pairs={{0,32},{1,33},{2,34},{3,35},{4,36},{5,37},{6,38},{7,39},{8,40},{9,... | collective-permute-start | bytes 15368 | tf_op jit(solution)/shard_map/ppermute | solution.py:26
  181.4 9.5 %collective-permute-start.8 = (f32[256,5]{0,1:T(8,128)S(1)}, f32[256,5]{0,1:T(8,128)S(1)}, u32[]{:S(2)}, u32[]{:S(2)}) collective-permute-start(f32[256,5]{0,1:T(8,128)S(1)} %get-tuple-element.16), channel_id=1, source_target_pairs={{0,32},{1,33},{2,34},{3,35},{4,36},{5,37},{6,38},{7,39},{8,40},{9,... | collective-permute-start | bytes 15368 | tf_op jit(solution)/shard_map/ppermute | solution.py:26
  196.5 0.7 copy-start.6
  196.5 0.7 copy-start.7
  196.5 210.4 %copy-start.4 = (bf16[4,5120]{1,0:T(4,128)(2,1)S(1)}, bf16[4,5120]{1,0:T(4,128)(2,1)}, u32[]{:S(2)}) copy-start(bf16[4,5120]{1,0:T(4,128)(2,1)} %param.17) | copy-start | bytes 122884
  196.6 290.2 %all-gather.7.cloned.1.call-start = ((), (), s32[]{:S(2)}) async-start(), calls=%async_computation.1 | async-start | bytes 2662400 | tf_op jit(solution)/shard_map/all_gather | solution.py:217
  408.7 290.4 %all-reduce.7.cloned.1.call-start = ((), (), s32[]{:S(2)}) async-start(), calls=%async_computation.3 | async-start | bytes 10485760
Sparse Core Ops, SparseCore 0:
  11.7 80.4 all-gather.4
  196.7 210.1 all-reduce.4
  410.2 76.4 all-gather.6
  503.2 195.8 all-reduce.6
where the time goes:
time: 709 us; the launch traced here: 707 us
  waiting for transfers between devices  578 us (82%)
  starting transfers between devices  40.5 us (6%)
  local copies, waits for them, and re-layouts  27.9 us (4%)
  other arithmetic  25.3 us (4%)
  matrix products  20.9 us (3%)
  between operations  14.8 us (2%)
    unnamed x6, waiting for transfers between devices  405 us
    all_gather x1, waiting for transfers between devices, per_device(): lax.all_gather(rms_scale(mixed_rows, mlp_gain), 'tp', axis=0, tiled=True)  78 us
    all_gather x1, waiting for transfers between devices, per_device(): lax.all_gather(normed, 'tp', axis=0, tiled=True)  61.6 us
    ppermute x12, waiting for transfers between devices, from_partner(): return lax.ppermute(value, axis, pairs)  33.9 us
    ppermute x12, starting transfers between devices, from_partner(): return lax.ppermute(value, axis, pairs)  33.1 us
    unnamed x22, local copies, waits for them, and re-layouts  17 us
  transfers between devices with their start and end apart: 17, of which 13 were waited for; matrix products, arithmetic and copies ran while one was open for 4% of the time, Pallas kernels for 0%

commit v1 on v0

--- a/solution.py
+++ b/solution.py
@@ -1,6 +1,8 @@
 import jax
 import jax.numpy as jnp
 from jax import lax
+from jax.experimental import pallas as pl
+from jax.experimental.pallas import tpu as pltpu
 from jax.sharding import PartitionSpec as P
 
 KEY_VALUE_HEADS = 8
@@ -13,6 +15,13 @@
 MAXP = 192
 REQUEST_PAGES = 8
 NEW_TOKEN_COUNT = 256
+NX, NZ = 4, 8
+ROWS = 4
+CLASS_ROWS = 128
+WIDTH = 5120
+HALF = WIDTH // 2
+MESH = pl.DeviceIdType.MESH
+BF16, F32 = jnp.bfloat16, jnp.float32
 
 
 EPSILON = 1e-06
@@ -30,14 +39,6 @@
     count = lax.axis_size(axis)
     pairs = [(source, (source + steps) % count) for source in range(count)]
     return lax.ppermute(value, axis, pairs)
-
-
-def rms_scale(values, gain_vec):
-    widened = values.astype(jnp.float32)
-    spread = jnp.mean(widened * widened, axis=-1, keepdims=True)
-    return (widened * lax.rsqrt(spread + EPSILON) * gain_vec.astype(jnp.float32)).astype(
-        jnp.bfloat16
-    )
 
 
 def rotary(values, positions):
@@ -55,7 +56,7 @@
 
 
 def token_info(lengths):
-    token_ids = jnp.arange(NEW_TOKEN_COUNT, dtype=jnp.int32)
+    token_ids = token_order()
     request_of = token_ids // SPAN
     offset_of = token_ids % SPAN
     positions = jnp.take(lengths, request_of) + offset_of
@@ -95,6 +96,392 @@
         & (new_pos[None, :] <= offset_of[:, None])
     )
     return old_ok | new_ok
+
+
+class Place:
+    def __init__(self):
+        me = lax.axis_index("tp")
+        self.x, self.z, self.c = me // 16, (me // 2) % NZ, me % 2
+
+    def at(self, dx=0, dz=0, flip=False):
+        x, z = (self.x + dx + NX) % NX, (self.z + dz + NZ) % NZ
+        c = 1 - self.c if flip else self.c
+        return {"tp": x * 16 + z * 2 + c}
+
+    def around(self):
+        return (
+            [self.at(dx=d) for d in range(1, NX)]
+            + [self.at(dz=d) for d in range(1, NZ)]
+            + [self.at(flip=True)]
+        )
+
+
+def remote(src, dst, send_sem, recv_sem, device):
+    return pltpu.make_async_remote_copy(
+        src_ref=src,
+        dst_ref=dst,
+        send_sem=send_sem,
+        recv_sem=recv_sem,
+        device_id=device,
+        device_id_type=MESH,
+    )
+
+
+def greet(place):
+    barrier = pltpu.get_barrier_semaphore()
+    peers = place.around()
+    for peer in peers:
+        pl.semaphore_signal(barrier, inc=1, device_id=peer, device_id_type=MESH)
+    return lambda: pl.semaphore_wait(barrier, len(peers))
+
+
+def rows_at(index, size):
+    return pl.ds(pl.multiple_of(index * size, size), size)
+
+
+def cols_at(half):
+    return pl.ds(half * HALF, HALF)
+
+
+GATHER_SCRATCH = [
+    pltpu.VMEM((NZ, ROWS, WIDTH), BF16),
+    pltpu.VMEM((32, WIDTH), F32),
+    pltpu.VMEM((2, CLASS_ROWS, WIDTH), BF16),
+    pltpu.SemaphoreType.DMA((24,)),
+    pltpu.SemaphoreType.DMA((24,)),
+    pltpu.SemaphoreType.DMA((2,)),
+]
+
+
+def gather_class(place, block, pieces, tile, gathered, send, recv, pair, along, cls):
+    first, second = ("x", "z") if along == "x" else ("z", "x")
+    n1, n2 = (NX, NZ) if along == "x" else (NZ, NX)
+    i1, i2 = (place.x, place.z) if along == "x" else (place.z, place.x)
+
+    def shift(axis, d):
+        return place.at(dx=d) if axis == "x" else place.at(dz=d)
+
+    pending = []
+    pieces[i1] = block
+    for d in range(1, n1):
+        copy = remote(pieces.at[i1], pieces.at[i1], send.at[d - 1], recv.at[d - 1], shift(first, d))
+        copy.start()
+        pending.append(copy)
+    for d in range(1, n1):
+        source = (i1 - d + n1) % n1
+        remote(
+            pieces.at[source], pieces.at[source], send.at[d - 1], recv.at[d - 1], shift(first, d)
+        ).wait_recv()
+    height = n1 * ROWS
+    for j in range(n1):
+        tile[j * ROWS : (j + 1) * ROWS, :] = pieces[j].astype(F32)
+    gathered[cls, rows_at(i2, height), :] = tile[0:height, :].astype(BF16)
+
+    partner = place.at(flip=True)
+
+    def to_partner(owner, half):
+        part = gathered.at[cls, rows_at(owner, height), cols_at(half)]
+        remote(part, part, pair.at[0], pair.at[1], partner).start()
+
+    steps = n2 // 2
+    for s in range(steps):
+        for half in range(2):
+            for side, sign in ((0, 1), (1, -1)):
+                owner = (i2 - sign * s + n2) % n2
+                part = gathered.at[cls, rows_at(owner, height), cols_at(half)]
+                slot = 7 + side * 8 + s * 2 + half
+                if s >= 1:
+                    before = slot - 2
+                    remote(
+                        part, part, send.at[before], recv.at[before], shift(second, sign)
+                    ).wait_recv()
+                if s < steps - 1 or half == side:
+                    copy = remote(part, part, send.at[slot], recv.at[slot], shift(second, sign))
+                    copy.start()
+                    pending.append(copy)
+                if s >= 1 or side == 0:
+                    to_partner(owner, half)
+    far = (i2 + steps) % n2
+    for side, sign in ((0, 1), (1, -1)):
+        part = gathered.at[cls, rows_at(far, height), cols_at(side)]
+        slot = 7 + side * 8 + (steps - 1) * 2 + side
+        remote(part, part, send.at[slot], recv.at[slot], shift(second, sign)).wait_recv()
+        to_partner(far, side)
+    for copy in pending:
+        copy.wait_send()
+
+
+def gather_rows(place, block, scratch):
+    pieces, tile, gathered, send, recv, pair = scratch
+
+    @pl.when(place.c == 0)
+    def _():
+        gather_class(place, block, pieces, tile, gathered, send, recv, pair, "x", 0)
+
+    @pl.when(place.c == 1)
+    def _():
+        gather_class(place, block, pieces, tile, gathered, send, recv, pair, "z", 1)
+
+
+def gather_pair_wait(place, scratch):
+    gathered, pair = scratch[2], scratch[5]
+    remote(
+        gathered.at[place.c], gathered.at[1 - place.c], pair.at[0], pair.at[1], place.at(flip=True)
+    ).wait()
+
+
+SCATTER_SCRATCH = [
+    pltpu.VMEM((CLASS_ROWS, WIDTH), BF16),
+    pltpu.VMEM((CLASS_ROWS, WIDTH), BF16),
+    pltpu.VMEM((CLASS_ROWS, WIDTH), F32),
+    pltpu.VMEM((8, 32, HALF), BF16),
+    pltpu.VMEM((8, 32, HALF), BF16),
+    pltpu.VMEM((32, WIDTH), F32),
+    pltpu.VMEM((NZ, ROWS, WIDTH), BF16),
+    pltpu.VMEM((NZ, ROWS, WIDTH), BF16),
+    pltpu.VMEM((NZ, ROWS, WIDTH), F32),
+    pltpu.VMEM((ROWS, WIDTH), F32),
+    pltpu.SemaphoreType.DMA((24,)),
+    pltpu.SemaphoreType.DMA((24,)),
+    pltpu.SemaphoreType.DMA((2,)),
+]
+
+
+def scatter_class(place, scratch, along):
+    _, swapped, own, outgoing, incoming, tile, leaving, arriving, parts, result, send, recv, _ = (
+        scratch
+    )
+    n1, n2 = (NZ, NX) if along == "z" else (NX, NZ)
+    i1, i2 = (place.z, place.x) if along == "z" else (place.x, place.z)
+    first, second = ("z", "x") if along == "z" else ("x", "z")
+    height = n2 * ROWS
+
+    def shift(axis, d):
+        return place.at(dx=d) if axis == "x" else place.at(dz=d)
+
+    def slot_of(ref, slot):
+        if height == 32:
+            return ref.at[slot]
+        return ref.at[slot // 2, pl.ds((slot % 2) * 16, 16)]
+
+    def mine(owner, half):
+        rows, cols = rows_at(owner, height), cols_at(half)
+        return own[rows, cols] + swapped[rows, cols].astype(F32)
+
+    steps = n1 // 2
+    pending = []
+
+    def hop(slot, sign):
+        return remote(
+            slot_of(outgoing, slot),
+            slot_of(incoming, slot),
+            send.at[slot],
+            recv.at[slot],
+            shift(first, sign),
+        )
+
+    for s in range(steps):
+        for half in range(2):
+            for side, sign in ((0, 1), (1, -1)):
+                begin = 0 if half == side else 1
+                if s < begin:
+                    continue
+                owner = (i1 + sign * (steps - s) + 2 * n1) % n1
+                slot = side * steps * 2 + s * 2 + half
+                value = mine(owner, half)
+                if s > begin:
+                    hop(slot - 2, sign).wait_recv()
+                    value = value + slot_of(incoming, slot - 2)[...].astype(F32)
+                slot_of(outgoing, slot)[...] = value.astype(BF16)
+                copy = hop(slot, sign)
+                copy.start()
+                pending.append(copy)
+    for half in range(2):
+        value = mine(i1, half)
+        for side, sign in ((0, 1), (1, -1)):
+            slot = side * steps * 2 + (steps - 1) * 2 + half
+            hop(slot, sign).wait_recv()
+            value = value + slot_of(incoming, slot)[...].astype(F32)
+        tile[0:height, cols_at(half)] = value
+
+    for j in range(n2):
+        part = tile[j * ROWS : (j + 1) * ROWS, :]
+        parts[j] = part
+        leaving[j] = part.astype(BF16)
+
+    def last(d):
+        return remote(
+            leaving.at[(i2 + d) % n2],
+            arriving.at[d],
+            send.at[16 + d],
+            recv.at[16 + d],
+            shift(second, d),
+        )
+
+    for d in range(1, n2):
+        copy = last(d)
+        copy.start()
+        pending.append(copy)
+    total = parts[i2]
+    for d in range(1, n2):
+        last(d).wait_recv()
+        total = total + arriving[d].astype(F32)
+    result[...] = total
+    for copy in pending:
+        copy.wait_send()
+
+
+def scatter_sums(place, partial, scratch):
+    handed, swapped, own = scratch[:3]
+    pair = scratch[12]
+    other = 1 - place.c
+    chunk = 1280
+
+    @pl.loop(0, WIDTH // chunk)
+    def _(k):
+        cols = pl.ds(pl.multiple_of(k * chunk, chunk), chunk)
+        handed[:, cols] = partial(other, cols).astype(BF16)
+        remote(
+            handed.at[:, cols], swapped.at[:, cols], pair.at[0], pair.at[1], place.at(flip=True)
+        ).start()
+
+    @pl.loop(0, WIDTH // chunk)
+    def _(k):
+        cols = pl.ds(pl.multiple_of(k * chunk, chunk), chunk)
+        own[:, cols] = partial(place.c, cols)
+
+    remote(handed, swapped, pair.at[0], pair.at[1], place.at(flip=True)).wait()
+
+    @pl.when(place.c == 0)
+    def _():
+        scatter_class(place, scratch, "z")
+
+    @pl.when(place.c == 1)
+    def _():
+        scatter_class(place, scratch, "x")
+
+    return scratch[9][...]
+
+
+def rms_block(values, gain_ref):
+    spread = jnp.mean(values * values, axis=-1, keepdims=True)
+    return (values * lax.rsqrt(spread + EPSILON) * gain_ref[...].astype(F32)).astype(BF16)
+
+
+def entry_kernel(stream, gain, weight, bias, projected, weight_buf, weight_sem, *gather):
+    place = Place()
+    ready = greet(place)
+    load = pltpu.make_async_copy(weight, weight_buf, weight_sem)
+    load.start()
+    block = rms_block(stream[...].astype(F32), gain)
+    ready()
+    gather_rows(place, block, gather)
+    load.wait()
+
+    def project(cls):
+        sums = jnp.dot(gather[2][cls], weight_buf[...], preferred_element_type=F32)
+        projected[cls] = (sums + bias[...].astype(F32)).astype(BF16)
+
+    project(place.c)
+    gather_pair_wait(place, gather)
+    project(1 - place.c)
+
+
+def exit_kernel(
+    attended, stream, gain, out_w, gate_w, up_w, down_w, layer_out,
+    out_buf, gate_buf, up_buf, down_buf, hidden, load_sems, *comm
+):
+    first, gather, second = comm[:13], comm[13:19], comm[19:]
+    place = Place()
+    ready = greet(place)
+    loads = [
+        pltpu.make_async_copy(src, dst, load_sems.at[k])
+        for k, (src, dst) in enumerate(
+            ((out_w, out_buf), (gate_w, gate_buf), (up_w, up_buf), (down_w, down_buf))
+        )
+    ]
+    for load in loads:
+        load.start()
+    loads[0].wait()
+    ready()
+
+    def out_term(cls, cols):
+        return jnp.dot(attended[cls], out_buf[:, cols], preferred_element_type=F32)
+
+    summed = scatter_sums(place, out_term, first)
+    mixed = (stream[...].astype(F32) + summed).astype(BF16)
+    block = rms_block(mixed.astype(F32), gain)
+    gather_rows(place, block, gather)
+    loads[1].wait()
+    loads[2].wait()
+
+    def hide(cls):
+        rows = gather[2][cls]
+        gate = jnp.dot(rows, gate_buf[...], preferred_element_type=F32)
+        up = jnp.dot(rows, up_buf[...], preferred_element_type=F32)
+        hidden[cls] = (gate / (1.0 + jnp.exp(-gate)) * up).astype(BF16)
+
+    hide(place.c)
+    gather_pair_wait(place, gather)
+    hide(1 - place.c)
+    loads[3].wait()
+
+    def down_term(cls, cols):
+        return jnp.dot(hidden[cls], down_buf[:, cols], preferred_element_type=F32)
+
+    summed = scatter_sums(place, down_term, second)
+    layer_out[...] = (mixed.astype(F32) + summed).astype(BF16)
+
+
+VM = pl.BlockSpec(memory_space=pltpu.VMEM)
+ANY = pl.BlockSpec(memory_space=pl.ANY)
+
+
+def entry(stream, gain, weight, bias):
+    columns = weight.shape[1]
+    return pl.pallas_call(
+        entry_kernel,
+        out_shape=jax.ShapeDtypeStruct((2, CLASS_ROWS, columns), BF16),
+        in_specs=[VM, VM, ANY, VM],
+        out_specs=VM,
+        scratch_shapes=[pltpu.VMEM(weight.shape, BF16), pltpu.SemaphoreType.DMA] + GATHER_SCRATCH,
+        compiler_params=pltpu.CompilerParams(collective_id=0, has_side_effects=True),
+        name="entry",
+    )(stream, gain[None], weight, bias[None])
+
+
+def leave(attended, stream, gain, out_w, gate_w, up_w, down_w):
+    buffers = [pltpu.VMEM(w.shape, BF16) for w in (out_w, gate_w, up_w, down_w)]
+    return pl.pallas_call(
+        exit_kernel,
+        out_shape=jax.ShapeDtypeStruct((ROWS, WIDTH), BF16),
+        in_specs=[VM, VM, VM, ANY, ANY, ANY, ANY],
+        out_specs=VM,
+        scratch_shapes=buffers
+        + [pltpu.VMEM((2, CLASS_ROWS, gate_w.shape[1]), BF16), pltpu.SemaphoreType.DMA((4,))]
+        + SCATTER_SCRATCH
+        + GATHER_SCRATCH
+        + SCATTER_SCRATCH,
+        compiler_params=pltpu.CompilerParams(
+            collective_id=1, has_side_effects=True, vmem_limit_bytes=60 * 2**20
+        ),
+        name="leave",
+    )(attended, stream, gain[None], out_w, gate_w, up_w, down_w)
+
+
+def token_order():
+    row = jnp.arange(CLASS_ROWS, dtype=jnp.int32)
+    z, x, r = row // 16, row // ROWS % NX, row % ROWS
+    zero = (x * 16 + z * 2) * ROWS + r
+    x, z = row // 32, row // ROWS % NZ
+    one = (x * 16 + z * 2 + 1) * ROWS + r
+    return jnp.concatenate([zero, one])
+
+
+def row_of_token(token):
+    device, r = token // ROWS, token % ROWS
+    x, z, c = device // 16, device // 2 % NZ, device % 2
+    return jnp.where(c == 0, z * 16 + x * ROWS, CLASS_ROWS + x * 32 + z * ROWS) + r
 
 
 def per_device(
@@ -126,16 +513,8 @@
     total_rows = tok_rows * device_total
     query_cols = query_weight.shape[2]
     proj_weight = jnp.concatenate([query_weight[:, 0, :], key_value_weight[:, 0, :]], axis=1)
-    proj_bias = jnp.concatenate([query_bias_input[0], key_value_bias[0]]).astype(jnp.float32)
-    normed = rms_scale(stream, attn_gain)
-    projected = (
-        jnp.dot(
-            lax.all_gather(normed, "tp", axis=0, tiled=True),
-            proj_weight,
-            preferred_element_type=jnp.float32,
-        )
-        + proj_bias
-    ).astype(jnp.bfloat16)
+    proj_bias = jnp.concatenate([query_bias_input[0], key_value_bias[0]])
+    projected = entry(stream, attn_gain, proj_weight, proj_bias).reshape(total_rows, -1)
     gathered = projected
     for each_level in range(level_count):
         partner = from_partner(gathered, "tp", group_flag + each_level)
@@ -169,7 +548,7 @@
     source_rows = (new_request * SPAN + new_page * PAGE_TOKENS)[:, None] + jnp.arange(
         PAGE_TOKENS, dtype=jnp.int32
     )[None, :]
-    fresh_pages = appended_rows[source_rows]
+    fresh_pages = appended_rows[row_of_token(source_rows)]
     local_cache = jnp.where((new_valid == 1)[:, None, None], fresh_pages, local_cache)
     updated_cache = local_cache[None]
     allowed = key_allowed(roles, lengths, request_of, offset_of, prompt_of)
@@ -206,25 +585,10 @@
     attn_piece = lax.dynamic_slice_in_dim(
         normalized, owner_index * query_cols, query_cols, 1
     ).astype(jnp.bfloat16)
-    out_rows = output_weight[0]
-    attn_sum = lax.psum_scatter(
-        jnp.dot(attn_piece, out_rows, preferred_element_type=jnp.float32),
-        "tp",
-        scatter_dimension=0,
-        tiled=True,
-    )
-    mixed_rows = (stream.astype(jnp.float32) + attn_sum).astype(jnp.bfloat16)
-    piece = lax.all_gather(rms_scale(mixed_rows, mlp_gain), "tp", axis=0, tiled=True)
-    gate_acts = jnp.dot(piece, w_gate, preferred_element_type=jnp.float32)
-    up_acts = jnp.dot(piece, w_up, preferred_element_type=jnp.float32)
-    hidden = (jax.nn.silu(gate_acts) * up_acts).astype(jnp.bfloat16)
-    mlp_sum = lax.psum_scatter(
-        jnp.dot(hidden, w_down, preferred_element_type=jnp.float32),
-        "tp",
-        scatter_dimension=0,
-        tiled=True,
-    )
-    layer_out = (mixed_rows.astype(jnp.float32) + mlp_sum).astype(jnp.bfloat16)
+    layer_out = leave(
+        attn_piece.reshape(2, CLASS_ROWS, query_cols),
+        stream, mlp_gain, output_weight[0], w_gate, w_up, w_down,
+    )
     return (layer_out, updated_cache)
 
 

time: 709 us -> 232 us (0.33)
  waiting for transfers between devices: 578 us -> 43.8 us
  Pallas kernels: 0 us -> 127 us
  matrix products: 20.9 us -> 2.38 us
  between operations: 14.8 us -> 1.07 us
  other arithmetic: 25.3 us -> 11.9 us
  starting transfers between devices: 40.5 us -> 27.9 us
  local copies, waits for them, and re-layouts: 27.9 us -> 17.7 us
    unnamed x6 -> x0, waiting for transfers between devices: 405 us -> none
    all_gather x2 -> x0, waiting for transfers between devices: 140 us -> none  [the longest x1 78 us: per_device(): lax.all_gather(rms_scale(mixed_rows, mlp_gain), 'tp', axis=0, tiled=True)]
    pallas_call x0 -> x2, Pallas kernels: none -> 127 us  [the longest x1 99.5 us: leave(): pl.pallas_call(exit_kernel, out_shape=jax.ShapeDtypeStruct((ROWS, WIDTH),...]
    dot_general x4 -> x0, matrix products: 18.5 us -> none  [the longest x1 7.74 us: per_device(): jnp.dot(hidden, w_down, preferred_element_type=jnp.float32)]
    ppermute x12, starting transfers between devices: 33.1 us -> 20.7 us  [from_partner(): return lax.ppermute(value, axis, pairs)]
    unnamed x22 -> x17, local copies, waits for them, and re-layouts: 17 us -> 6.96 us
    ppermute x12, waiting for transfers between devices: 33.9 us -> 43.8 us  [from_partner(): return lax.ppermute(value, axis, pairs)]
  transfers between devices with their start and end apart: 17 -> 13, of which waited for: 13 -> 8; matrix products, arithmetic and copies ran while one was open for 4% -> 8% of each run, Pallas kernels for 0% -> 12%
where the time goes in v1:
time: 232 us; the launch traced here: 231 us
  Pallas kernels  127 us (55%)
  waiting for transfers between devices  43.8 us (19%)
  starting transfers between devices  27.9 us (12%)
  local copies, waits for them, and re-layouts  17.7 us (8%)
  other arithmetic  11.9 us (5%)
  matrix products  2.38 us (1%)
    pallas_call x1, Pallas kernels, leave(): pl.pallas_call(exit_kernel, out_shape=jax.ShapeDtypeStruct((ROWS, WIDTH),...  99.5 us
    ppermute x12, waiting for transfers between devices, from_partner(): return lax.ppermute(value, axis, pairs)  43.8 us
    pallas_call x1, Pallas kernels, entry(): pl.pallas_call(entry_kernel, out_shape=jax.ShapeDtypeStruct((2, CLASS_ROW...  27 us
    ppermute x12, starting transfers between devices, from_partner(): return lax.ppermute(value, axis, pairs)  20.7 us
    ppermute x1, starting transfers between devices, passed_along(): return lax.ppermute(value, axis, pairs)  7.27 us
    unnamed x17, local copies, waits for them, and re-layouts  6.96 us
  transfers between devices with their start and end apart: 13, of which 8 were waited for; matrix products, arithmetic and copies ran while one was open for 8% of the time, Pallas kernels for 12%

profile of v1, /device:TPU:16, one launch (start us, length us, event | category | flops | bytes accessed | tf_op | source)
XLA Modules:
  0.0 231.3 jit_solution(4091766754613487325)
XLA Ops:
  0.7 1.1 copy.75
  3.0 7.3 %collective-permute-start.3 = (bf16[8,16,256]{2,1,0:T(8,128)(2,1)S(1)}, bf16[8,16,256]{2,1,0:T(8,128)(2,1)S(1)}, u32[]{:S(2)}, u32[]{:S(2)}) collective-permute-start(bf16[8,16,256]{2,1,0:T(8,128)(2,1)S(1)} %gather_fusion.1), channel_id=1, source_target_pairs={{0,8},{1,9},{2,10},{3,11},{4,12},{5,13},{6,14},{7,15},{8,16},{9,17... | collective-permute-start | bytes 196616 | tf_op jit(solution)/shard_map/ppermute | solution.py:41
  10.2 1.3 broadcast_in_dim.53.gain
  11.6 1.7 copy.53
  13.3 1.6 copy.54
  14.9 1.3 maximum_bitcast_fusion.1.bias
  16.1 1.8 pad_maximum_fusion.weight
  17.9 27.0 %entry.1 = bf16[2,128,112]{2,1,0:T(8,128)(2,1)} custom-call(bf16[4,5120]{1,0:T(4,128)(2,1)} %stream.3, bf16[1,5120]{1,0:T(2,128)(2,1)} %broadcast_in_dim.53.gain, bf16[5120,112]{1,0:T(8,128)(2,1)} %pad_maximum_fusion.weight, bf16[1,112]{1,0:T(2,128)(2,1)} %maximum_bitcast_fusion.1.bias), custom_call_target="tpu_custom_call" | custom-call | tf_op jit(solution)/shard_map/entry/pallas_call | solution.py:442
  44.9 0.9 copy.55
  45.8 2.8 %collective-permute-start = (bf16[256,112]{0,1:T(8,128)(2,1)S(1)}, bf16[256,112]{0,1:T(8,128)(2,1)S(1)}, u32[]{:S(2)}, u32[]{:S(2)}) collective-permute-start(bf16[256,112]{0,1:T(8,128)(2,1)S(1)} %copy.55), channel_id=1, source_target_pairs={{0,8},{1,9},{2,10},{3,11},{4,12},{5,13},{6,14},{7,15},{8,0},{9,1},... | collective-permute-start | bytes 172040 | tf_op jit(solution)/shard_map/ppermute | solution.py:35
  49.6 1.3 and_select_fusion.1
  51.9 1.3 compare_select_fusion.6
  53.8 1.3 and_or_fusion
  55.7 0.9 copy.58
  57.3 3.3 %collective-permute-done.1 = bf16[256,224]{0,1:T(8,128)(2,1)S(1)} collective-permute-done((bf16[256,224]{0,1:T(8,128)(2,1)S(1)}, bf16[256,224]{0,1:T(8,128)(2,1)S(1)}, u32[]{:S(2)}, u32[]{:S(2)}) %collective-permute-start.1) | collective-permute-done | bytes 114720 | tf_op jit(solution)/shard_map/ppermute | solution.py:35
  60.7 1.3 collective-permute-start.2
  62.0 0.7 scatter_fusion
  62.8 6.2 %collective-permute-done.2 = bf16[256,448]{0,1:T(8,128)(2,1)S(1)} collective-permute-done((bf16[256,448]{0,1:T(8,128)(2,1)S(1)}, bf16[256,448]{0,1:T(8,128)(2,1)S(1)}, u32[]{:S(2)}, u32[]{:S(2)}) %collective-permute-start.2) | collective-permute-done | bytes 229408 | tf_op jit(solution)/shard_map/ppermute | solution.py:35
  70.2 3.9 %gather_fusion = bf16[1024,256]{1,0:T(8,128)(2,1)S(1)} fusion(bf16[256,256]{1,0:T(8,128)(2,1)S(1)} %copy.60, s32[1024]{0:T(1024)S(1)} %broadcast_clamp_fusion), kind=kCustom, calls=%fused_computation | custom fusion | bytes 1052672 | tf_op jit(solution)/shard_map/gather | solution.py:551
  74.5 1.1 fusion
  75.6 1.2 fusion.5
  76.9 3.5 %collective-permute-start.5 = (f32[256,640]{0,1:T(8,128)S(1)}, f32[256,640]{0,1:T(8,128)S(1)}, u32[]{:S(2)}, u32[]{:S(2)}) collective-permute-start(f32[256,640]{0,1:T(8,128)S(1)} %bitcast.113), channel_id=1, source_target_pairs={{0,8},{1,9},{2,10},{3,11},{4,12},{5,13},{6,14},{7,15},{8,0},{9,1},... | collective-permute-start | bytes 1966088 | tf_op jit(solution)/shard_map/ppermute | solution.py:35
  80.4 1.1 fusion.3
  81.5 2.8 %collective-permute-start.10 = (f32[256,5]{0,1:T(8,128)S(1)}, f32[256,5]{0,1:T(8,128)S(1)}, u32[]{:S(2)}, u32[]{:S(2)}) collective-permute-start(f32[256,5]{0,1:T(8,128)S(1)} %bitcast.125), channel_id=1, source_target_pairs={{0,8},{1,9},{2,10},{3,11},{4,12},{5,13},{6,14},{7,15},{8,0},{9,1},... | collective-permute-start | bytes 15368 | tf_op jit(solution)/shard_map/ppermute | solution.py:35
  84.3 3.2 %collective-permute-start.4 = (f32[256,5]{0,1:T(8,128)S(1)}, f32[256,5]{0,1:T(8,128)S(1)}, u32[]{:S(2)}, u32[]{:S(2)}) collective-permute-start(f32[256,5]{0,1:T(8,128)S(1)} %bitcast.124), channel_id=1, source_target_pairs={{0,8},{1,9},{2,10},{3,11},{4,12},{5,13},{6,14},{7,15},{8,0},{9,1},... | collective-permute-start | bytes 15368 | tf_op jit(solution)/shard_map/ppermute | solution.py:35
  87.5 11.3 %collective-permute-done.10 = f32[256,5]{0,1:T(8,128)S(1)} collective-permute-done((f32[256,5]{0,1:T(8,128)S(1)}, f32[256,5]{0,1:T(8,128)S(1)}, u32[]{:S(2)}, u32[]{:S(2)}) %collective-permute-start.10) | collective-permute-done | bytes 5152 | tf_op jit(solution)/shard_map/ppermute | solution.py:35
  99.7 1.4 collective-permute-start.11
  101.7 12.7 %collective-permute-done.11 = f32[256,5]{0,1:T(8,128)S(1)} collective-permute-done((f32[256,5]{0,1:T(8,128)S(1)}, f32[256,5]{0,1:T(8,128)S(1)}, u32[]{:S(2)}, u32[]{:S(2)}) %collective-permute-start.11) | collective-permute-done | bytes 5152 | tf_op jit(solution)/shard_map/ppermute | solution.py:35
  115.3 3.0 %collective-permute-start.12 = (f32[256,5]{0,1:T(8,128)S(1)}, f32[256,5]{0,1:T(8,128)S(1)}, u32[]{:S(2)}, u32[]{:S(2)}) collective-permute-start(f32[256,5]{0,1:T(8,128)S(1)} %get-tuple-element.11), channel_id=1, source_target_pairs={{0,32},{1,33},{2,34},{3,35},{4,36},{5,37},{6,38},{7,39},{8,40},{9,... | collective-permute-start | bytes 15368 | tf_op jit(solution)/shard_map/ppermute | solution.py:35
  119.4 9.9 %collective-permute-done.12 = f32[256,5]{0,1:T(8,128)S(1)} collective-permute-done((f32[256,5]{0,1:T(8,128)S(1)}, f32[256,5]{0,1:T(8,128)S(1)}, u32[]{:S(2)}, u32[]{:S(2)}) %collective-permute-start.12) | collective-permute-done | bytes 5152 | tf_op jit(solution)/shard_map/ppermute | solution.py:35
  130.3 99.5 %leave.1 = bf16[4,5120]{1,0:T(4,128)(2,1)} custom-call(bf16[2,128,80]{2,1,0:T(8,128)(2,1)} %bitcast.121, bf16[4,5120]{1,0:T(4,128)(2,1)} %stream.3, bf16[1,5120]{1,0:T(2,128)(2,1)} %broadcast_in_dim.69.gain, bf16[80,5120]{1,0:T(8,128)(2,1)} %bitcast.111, bf16[5120,256]{1,0:T(8,128)(2,1)} %gate_w.1, bf16[5120,256]{1,0:T(8,128)(2,1)} %up_w.1, ...), custom_call_target="tpu_custom_call" | custom-call | tf_op jit(solution)/shard_map/leave/pallas_call | solution.py:455
  229.8 1.4 copy.76
  (80 shorter events, 10.9 us)
Async XLA Ops:
  0.6 48.0 %copy-start.3 = (s32[2]{0:T(128)S(1)}, s32[2]{0:T(128)}, u32[]{:S(2)}) copy-start(s32[2]{0:T(128)} %param.29) | copy-start | bytes 28
  0.6 48.6 %copy-start.2 = (s32[2,192]{1,0:T(2,128)S(1)}, s32[2,192]{1,0:T(2,128)}, u32[]{:S(2)}) copy-start(s32[2,192]{1,0:T(2,128)} %param.30) | copy-start | bytes 4612
  0.7 48.9 %copy-start.4 = (s32[2,8]{1,0:T(2,128)S(1)}, s32[2,8]{1,0:T(2,128)}, u32[]{:S(2)}) copy-start(s32[2,8]{1,0:T(2,128)} %param.31) | copy-start | bytes 196
  3.0 59.0 %collective-permute-start.3 = (bf16[8,16,256]{2,1,0:T(8,128)(2,1)S(1)}, bf16[8,16,256]{2,1,0:T(8,128)(2,1)S(1)}, u32[]{:S(2)}, u32[]{:S(2)}) collective-permute-start(bf16[8,16,256]{2,1,0:T(8,128)(2,1)S(1)} %gather_fusion.1), channel_id=1, source_target_pairs={{0,8},{1,9},{2,10},{3,11},{4,12},{5,13},{6,14},{7,15},{8,16},{9,17... | collective-permute-start | bytes 196616 | tf_op jit(solution)/shard_map/ppermute | solution.py:41
  45.8 9.5 %collective-permute-start = (bf16[256,112]{0,1:T(8,128)(2,1)S(1)}, bf16[256,112]{0,1:T(8,128)(2,1)S(1)}, u32[]{:S(2)}, u32[]{:S(2)}) collective-permute-start(bf16[256,112]{0,1:T(8,128)(2,1)S(1)} %copy.55), channel_id=1, source_target_pairs={{0,8},{1,9},{2,10},{3,11},{4,12},{5,13},{6,14},{7,15},{8,0},{9,1},... | collective-permute-start | bytes 172040 | tf_op jit(solution)/shard_map/ppermute | solution.py:35
  55.4 5.2 %collective-permute-start.1 = (bf16[256,224]{0,1:T(8,128)(2,1)S(1)}, bf16[256,224]{0,1:T(8,128)(2,1)S(1)}, u32[]{:S(2)}, u32[]{:S(2)}) collective-permute-start(bf16[256,224]{0,1:T(8,128)(2,1)S(1)} %maximum_select_fusion.3), channel_id=1, source_target_pairs={{0,16},{1,17},{2,18},{3,19},{4,20},{5,21},{6,22},{7,23},{8,24},{9,... | collective-permute-start | bytes 344072 | tf_op jit(solution)/shard_map/ppermute | solution.py:35
  60.7 8.3 %collective-permute-start.2 = (bf16[256,448]{0,1:T(8,128)(2,1)S(1)}, bf16[256,448]{0,1:T(8,128)(2,1)S(1)}, u32[]{:S(2)}, u32[]{:S(2)}) collective-permute-start(bf16[256,448]{0,1:T(8,128)(2,1)S(1)} %maximum_select_fusion.1), channel_id=1, source_target_pairs={{0,32},{1,33},{2,34},{3,35},{4,36},{5,37},{6,38},{7,39},{8,40},{9,... | collective-permute-start | bytes 688136 | tf_op jit(solution)/shard_map/ppermute | solution.py:35
  74.3 2.6 %copy-start = (bf16[64,16,256]{2,1,0:T(8,128)(2,1)}, bf16[64,16,256]{2,1,0:T(8,128)(2,1)S(1)}, u32[]{:S(2)}) copy-start(bf16[64,16,256]{2,1,0:T(8,128)(2,1)S(1)} %broadcast_select_fusion) | copy-start | bytes 1572868
  76.9 41.9 %copy-start.1 = (bf16[5120]{0:T(1024)(128)(2,1)S(1)}, bf16[5120]{0:T(1024)(128)(2,1)}, u32[]{:S(2)}) copy-start(bf16[5120]{0:T(1024)(128)(2,1)} %param.24) | copy-start | bytes 30724
  76.9 22.0 %collective-permute-start.5 = (f32[256,640]{0,1:T(8,128)S(1)}, f32[256,640]{0,1:T(8,128)S(1)}, u32[]{:S(2)}, u32[]{:S(2)}) collective-permute-start(f32[256,640]{0,1:T(8,128)S(1)} %bitcast.113), channel_id=1, source_target_pairs={{0,8},{1,9},{2,10},{3,11},{4,12},{5,13},{6,14},{7,15},{8,0},{9,1},... | collective-permute-start | bytes 1966088 | tf_op jit(solution)/shard_map/ppermute | solution.py:35
  81.5 17.3 %collective-permute-start.10 = (f32[256,5]{0,1:T(8,128)S(1)}, f32[256,5]{0,1:T(8,128)S(1)}, u32[]{:S(2)}, u32[]{:S(2)}) collective-permute-start(f32[256,5]{0,1:T(8,128)S(1)} %bitcast.125), channel_id=1, source_target_pairs={{0,8},{1,9},{2,10},{3,11},{4,12},{5,13},{6,14},{7,15},{8,0},{9,1},... | collective-permute-start | bytes 15368 | tf_op jit(solution)/shard_map/ppermute | solution.py:35
  84.3 14.6 %collective-permute-start.4 = (f32[256,5]{0,1:T(8,128)S(1)}, f32[256,5]{0,1:T(8,128)S(1)}, u32[]{:S(2)}, u32[]{:S(2)}) collective-permute-start(f32[256,5]{0,1:T(8,128)S(1)} %bitcast.124), channel_id=1, source_target_pairs={{0,8},{1,9},{2,10},{3,11},{4,12},{5,13},{6,14},{7,15},{8,0},{9,1},... | collective-permute-start | bytes 15368 | tf_op jit(solution)/shard_map/ppermute | solution.py:35
  99.0 15.6 %collective-permute-start.7 = (f32[256,640]{0,1:T(8,128)S(1)}, f32[256,640]{0,1:T(8,128)S(1)}, u32[]{:S(2)}, u32[]{:S(2)}) collective-permute-start(f32[256,640]{0,1:T(8,128)S(1)} %bitcast.106), channel_id=1, source_target_pairs={{0,16},{1,17},{2,18},{3,19},{4,20},{5,21},{6,22},{7,23},{8,24},{9,... | collective-permute-start | bytes 1966088 | tf_op jit(solution)/shard_map/ppermute | solution.py:35
  99.7 14.7 %collective-permute-start.11 = (f32[256,5]{0,1:T(8,128)S(1)}, f32[256,5]{0,1:T(8,128)S(1)}, u32[]{:S(2)}, u32[]{:S(2)}) collective-permute-start(f32[256,5]{0,1:T(8,128)S(1)} %get-tuple-element.15), channel_id=1, source_target_pairs={{0,16},{1,17},{2,18},{3,19},{4,20},{5,21},{6,22},{7,23},{8,24},{9,... | collective-permute-start | bytes 15368 | tf_op jit(solution)/shard_map/ppermute | solution.py:35
  101.1 13.5 %collective-permute-start.6 = (f32[256,5]{0,1:T(8,128)S(1)}, f32[256,5]{0,1:T(8,128)S(1)}, u32[]{:S(2)}, u32[]{:S(2)}) collective-permute-start(f32[256,5]{0,1:T(8,128)S(1)} %get-tuple-element.18), channel_id=1, source_target_pairs={{0,16},{1,17},{2,18},{3,19},{4,20},{5,21},{6,22},{7,23},{8,24},{9,... | collective-permute-start | bytes 15368 | tf_op jit(solution)/shard_map/ppermute | solution.py:35
  114.7 14.7 %collective-permute-start.9 = (f32[256,640]{0,1:T(8,128)S(1)}, f32[256,640]{0,1:T(8,128)S(1)}, u32[]{:S(2)}, u32[]{:S(2)}) collective-permute-start(f32[256,640]{0,1:T(8,128)S(1)} %bitcast.105), channel_id=1, source_target_pairs={{0,32},{1,33},{2,34},{3,35},{4,36},{5,37},{6,38},{7,39},{8,40},{9,... | collective-permute-start | bytes 1966088 | tf_op jit(solution)/shard_map/ppermute | solution.py:35
  115.3 14.1 %collective-permute-start.12 = (f32[256,5]{0,1:T(8,128)S(1)}, f32[256,5]{0,1:T(8,128)S(1)}, u32[]{:S(2)}, u32[]{:S(2)}) collective-permute-start(f32[256,5]{0,1:T(8,128)S(1)} %get-tuple-element.11), channel_id=1, source_target_pairs={{0,32},{1,33},{2,34},{3,35},{4,36},{5,37},{6,38},{7,39},{8,40},{9,... | collective-permute-start | bytes 15368 | tf_op jit(solution)/shard_map/ppermute | solution.py:35
  118.3 11.1 %collective-permute-start.8 = (f32[256,5]{0,1:T(8,128)S(1)}, f32[256,5]{0,1:T(8,128)S(1)}, u32[]{:S(2)}, u32[]{:S(2)}) collective-permute-start(f32[256,5]{0,1:T(8,128)S(1)} %get-tuple-element.14), channel_id=1, source_target_pairs={{0,32},{1,33},{2,34},{3,35},{4,36},{5,37},{6,38},{7,39},{8,40},{9,... | collective-permute-start | bytes 15368 | tf_op jit(solution)/shard_map/ppermute | solution.py:35

commit v2 on v1

v2 whole, which is shorter than its diff:
```python
import math

import jax
import jax.numpy as jnp
from jax import lax
from jax.experimental import pallas as pl
from jax.experimental.pallas import tpu as pltpu
from jax.sharding import PartitionSpec as P

KEY_VALUE_HEADS = 8
HEAD_SIZE = 128
SPAN = 128
PAGE_TOKENS = 16
QUERY_PER_KV = 5
REQUEST_PAGES = 8
TOKENS = 256
OWNERS = 8
SLOTS = 64
KEYS = SLOTS * PAGE_TOKENS
MIGRATED = 8
Q_COLS, KV_COLS = 80, 32
PACK = 96
NX, NZ = 4, 8
ROWS = 4
CLASS_ROWS = 128
WIDTH = 5120
HALF = WIDTH // 2
MESH = pl.DeviceIdType.MESH
BF16, F32 = jnp.bfloat16, jnp.float32


EPSILON = 1e-06
ROPE_BASE = 1000000.0
NEG_LARGE = -1e30
LOG_BASE = math.log(ROPE_BASE)


class Place:
    def __init__(self):
        me = lax.axis_index("tp")
        self.x, self.z, self.c = me // 16, (me // 2) % NZ, me % 2

    def at(self, dx=0, dz=0, flip=False):
        x, z = (self.x + dx + NX) % NX, (self.z + dz + NZ) % NZ
        c = 1 - self.c if flip else self.c
        return {"tp": x * 16 + z * 2 + c}

    def owner(self):
        return self.x * 2 + self.z // 4

    def around(self):
        return (
            [self.at(dx=d) for d in range(1, NX)]
            + [self.at(dz=d) for d in range(1, NZ)]
            + [self.at(flip=True)]
        )


def remote(src, dst, send_sem, recv_sem, device):
    return pltpu.make_async_remote_copy(
        src_ref=src,
        dst_ref=dst,
        send_sem=send_sem,
        recv_sem=recv_sem,
        device_id=device,
        device_id_type=MESH,
    )


def greet(place, more=()):
    barrier = pltpu.get_barrier_semaphore()
    peers = place.around() + list(more)
    for peer in peers:
        pl.semaphore_signal(barrier, inc=1, device_id=peer, device_id_type=MESH)
    return lambda: pl.semaphore_wait(barrier, len(peers))


def rows_at(index, size):
    return pl.ds(pl.multiple_of(index * size, size), size)


def cols_at(half):
    return pl.ds(half * HALF, HALF)


GATHER_SCRATCH = [
    pltpu.VMEM((NZ, ROWS, WIDTH), BF16),
    pltpu.VMEM((32, WIDTH), F32),
    pltpu.VMEM((2, CLASS_ROWS, WIDTH), BF16),
    pltpu.SemaphoreType.DMA((24,)),
    pltpu.SemaphoreType.DMA((24,)),
    pltpu.SemaphoreType.DMA((2,)),
]


def gather_class(place, block, pieces, tile, gathered, send, recv, pair, along, cls, extra):
    first, second = ("x", "z") if along == "x" else ("z", "x")
    n1, n2 = (NX, NZ) if along == "x" else (NZ, NX)
    i1, i2 = (place.x, place.z) if along == "x" else (place.z, place.x)

    def shift(axis, d):
        return place.at(dx=d) if axis == "x" else place.at(dz=d)

    pending = []
    pieces[i1] = block
    for d in range(1, n1):
        copy = remote(pieces.at[i1], pieces.at[i1], send.at[d - 1], recv.at[d - 1], shift(first, d))
        copy.start()
        pending.append(copy)
    extra()
    for d in range(1, n1):
        source = (i1 - d + n1) % n1
        remote(
            pieces.at[source], pieces.at[source], send.at[d - 1], recv.at[d - 1], shift(first, d)
        ).wait_recv()
    height = n1 * ROWS
    for j in range(n1):
        tile[j * ROWS : (j + 1) * ROWS, :] = pieces[j].astype(F32)
    gathered[cls, rows_at(i2, height), :] = tile[0:height, :].astype(BF16)

    partner = place.at(flip=True)

    def to_partner(owner, half):
        part = gathered.at[cls, rows_at(owner, height), cols_at(half)]
        remote(part, part, pair.at[0], pair.at[1], partner).start()

    steps = n2 // 2
    for s in range(steps):
        for half in range(2):
            for side, sign in ((0, 1), (1, -1)):
                owner = (i2 - sign * s + n2) % n2
                part = gathered.at[cls, rows_at(owner, height), cols_at(half)]
                slot = 7 + side * 8 + s * 2 + half
                if s >= 1:
                    before = slot - 2
                    remote(
                        part, part, send.at[before], recv.at[before], shift(second, sign)
                    ).wait_recv()
                if s < steps - 1 or half == side:
                    copy = remote(part, part, send.at[slot], recv.at[slot], shift(second, sign))
                    copy.start()
                    pending.append(copy)
                if s >= 1 or side == 0:
                    to_partner(owner, half)
    far = (i2 + steps) % n2
    for side, sign in ((0, 1), (1, -1)):
        part = gathered.at[cls, rows_at(far, height), cols_at(side)]
        slot = 7 + side * 8 + (steps - 1) * 2 + side
        remote(part, part, send.at[slot], recv.at[slot], shift(second, sign)).wait_recv()
        to_partner(far, side)
    for copy in pending:
        copy.wait_send()


def gather_rows(place, block, scratch, extra=lambda: None):
    pieces, tile, gathered, send, recv, pair = scratch

    @pl.when(place.c == 0)
    def _():
        gather_class(place, block, pieces, tile, gathered, send, recv, pair, "x", 0, extra)

    @pl.when(place.c == 1)
    def _():
        gather_class(place, block, pieces, tile, gathered, send, recv, pair, "z", 1, extra)


def gather_pair_wait(place, scratch):
    gathered, pair = scratch[2], scratch[5]
    remote(
        gathered.at[place.c], gathered.at[1 - place.c], pair.at[0], pair.at[1], place.at(flip=True)
    ).wait()


SCATTER_SCRATCH = [
    pltpu.VMEM((CLASS_ROWS, WIDTH), BF16),
    pltpu.VMEM((CLASS_ROWS, WIDTH), BF16),
    pltpu.VMEM((CLASS_ROWS, WIDTH), F32),
    pltpu.VMEM((8, 32, HALF), BF16),
    pltpu.VMEM((8, 32, HALF), BF16),
    pltpu.VMEM((32, WIDTH), F32),
    pltpu.VMEM((NZ, ROWS, WIDTH), BF16),
    pltpu.VMEM((NZ, ROWS, WIDTH), BF16),
    pltpu.VMEM((NZ, ROWS, WIDTH), F32),
    pltpu.VMEM((ROWS, WIDTH), F32),
    pltpu.SemaphoreType.DMA((24,)),
    pltpu.SemaphoreType.DMA((24,)),
    pltpu.SemaphoreType.DMA((2,)),
]


def scatter_class(place, scratch, along):
    _, swapped, own, outgoing, incoming, tile, leaving, arriving, parts, result, send, recv, _ = (
        scratch
    )
    n1, n2 = (NZ, NX) if along == "z" else (NX, NZ)
    i1, i2 = (place.z, place.x) if along == "z" else (place.x, place.z)
    first, second = ("z", "x") if along == "z" else ("x", "z")
    height = n2 * ROWS

    def shift(axis, d):
        return place.at(dx=d) if axis == "x" else place.at(dz=d)

    def slot_of(ref, slot):
        if height == 32:
            return ref.at[slot]
        return ref.at[slot // 2, pl.ds((slot % 2) * 16, 16)]

    def mine(owner, half):
        rows, cols = rows_at(owner, height), cols_at(half)
        return own[rows, cols] + swapped[rows, cols].astype(F32)

    steps = n1 // 2
    pending = []

    def hop(slot, sign):
        return remote(
            slot_of(outgoing, slot),
            slot_of(incoming, slot),
            send.at[slot],
            recv.at[slot],
            shift(first, sign),
        )

    for s in range(steps):
        for half in range(2):
            for side, sign in ((0, 1), (1, -1)):
                begin = 0 if half == side else 1
                if s < begin:
                    continue
                owner = (i1 + sign * (steps - s) + 2 * n1) % n1
                slot = side * steps * 2 + s * 2 + half
                value = mine(owner, half)
                if s > begin:
                    hop(slot - 2, sign).wait_recv()
                    value = value + slot_of(incoming, slot - 2)[...].astype(F32)
                slot_of(outgoing, slot)[...] = value.astype(BF16)
                copy = hop(slot, sign)
                copy.start()
                pending.append(copy)
    for half in range(2):
        value = mine(i1, half)
        for side, sign in ((0, 1), (1, -1)):
            slot = side * steps * 2 + (steps - 1) * 2 + half
            hop(slot, sign).wait_recv()
            value = value + slot_of(incoming, slot)[...].astype(F32)
        tile[0:height, cols_at(half)] = value

    for j in range(n2):
        part = tile[j * ROWS : (j + 1) * ROWS, :]
        parts[j] = part
        leaving[j] = part.astype(BF16)

    def last(d):
        return remote(
            leaving.at[(i2 + d) % n2],
            arriving.at[d],
            send.at[16 + d],
            recv.at[16 + d],
            shift(second, d),
        )

    for d in range(1, n2):
        copy = last(d)
        copy.start()
        pending.append(copy)
    total = parts[i2]
    for d in range(1, n2):
        last(d).wait_recv()
        total = total + arriving[d].astype(F32)
    result[...] = total
    for copy in pending:
        copy.wait_send()


def scatter_sums(place, partial, scratch):
    handed, swapped, own = scratch[:3]
    pair = scratch[12]
    other = 1 - place.c
    chunk = 1280

    @pl.loop(0, WIDTH // chunk)
    def _(k):
        cols = pl.ds(pl.multiple_of(k * chunk, chunk), chunk)
        handed[:, cols] = partial(other, cols).astype(BF16)
        remote(
            handed.at[:, cols], swapped.at[:, cols], pair.at[0], pair.at[1], place.at(flip=True)
        ).start()

    @pl.loop(0, WIDTH // chunk)
    def _(k):
        cols = pl.ds(pl.multiple_of(k * chunk, chunk), chunk)
        own[:, cols] = partial(place.c, cols)

    remote(handed, swapped, pair.at[0], pair.at[1], place.at(flip=True)).wait()

    @pl.when(place.c == 0)
    def _():
        scatter_class(place, scratch, "z")

    @pl.when(place.c == 1)
    def _():
        scatter_class(place, scratch, "x")

    return scratch[9][...]


def rms_block(values, gain_ref):
    spread = jnp.mean(values * values, axis=-1, keepdims=True)
    lines = gain_ref[...].astype(F32)
    gain = jnp.concatenate([lines[k : k + 1] for k in range(WIDTH // 128)], axis=1)
    return (values * lax.rsqrt(spread + EPSILON) * gain).astype(BF16)


def across(a, b):
    return lax.dot_general(a, b, (((1,), (1,)), ((), ())), preferred_element_type=F32)


def entry_kernel(
    stream, gain, query_w, kv_w, query_b, kv_b, cache, mig_from, pieces, landed,
    weight_buf, cache_buf, leaving, load_sems, page_sems, send, recv, *gather
):
    place = Place()
    owner = place.owner()
    side = place.z // 4
    ready = greet(place, (place.at(dx=1, dz=4), place.at(dx=-1, dz=4)))
    loads = [
        pltpu.make_async_copy(query_w, weight_buf.at[0:Q_COLS], load_sems.at[0]),
        pltpu.make_async_copy(kv_w, weight_buf.at[Q_COLS : Q_COLS + KV_COLS], load_sems.at[1]),
        pltpu.make_async_copy(cache, cache_buf, load_sems.at[2]),
    ]
    for load in loads:
        load.start()
    weight_buf[Q_COLS + KV_COLS :, :] = jnp.zeros((128 - Q_COLS - KV_COLS, WIDTH), BF16)
    block = rms_block(stream[...].astype(F32), gain)
    ready()
    pages = remote(leaving, landed, page_sems.at[0], page_sems.at[1], place.at(dx=side, dz=4))

    def send_pages():
        loads[2].wait()
        for j in range(MIGRATED):
            leaving[j] = cache_buf[mig_from[owner, j]]
        pages.start()

    gather_rows(place, block, gather, send_pages)
    loads[0].wait()
    loads[1].wait()
    bias = jnp.concatenate(
        [
            query_b[...].astype(F32),
            kv_b[...].astype(F32),
            jnp.zeros((1, 128 - Q_COLS - KV_COLS), F32),
        ],
        axis=1,
    )
    pending = []

    def part(who, cls, slot, device):
        ref = pieces.at[who, cls]
        return remote(ref, ref, send.at[slot], recv.at[slot], device)

    def project(cls, base):
        pieces[owner, cls] = (across(gather[2][cls], weight_buf[...]) + bias).astype(BF16)
        for k, device in enumerate([place.at(dz=4)] + [place.at(dx=d) for d in range(1, NX)]):
            copy = part(owner, cls, base + k, device)
            copy.start()
            pending.append(copy)

    project(place.c, 0)
    gather_pair_wait(place, gather)
    project(1 - place.c, 4)
    opposite = place.x * 2 + 1 - side
    for k, cls in enumerate((place.c, 1 - place.c)):
        part(opposite, cls, 4 * k, place.at(dz=4)).wait_recv()
        for d in range(1, NX):
            copy = part(opposite, cls, 8 + 3 * k + d - 1, place.at(dx=d))
            copy.start()
            pending.append(copy)
    for d in range(1, NX):
        x = (place.x - d + NX) % NX
        for k, cls in enumerate((place.c, 1 - place.c)):
            part(x * 2 + side, cls, 4 * k + d, place.at(dx=d)).wait_recv()
            part(x * 2 + 1 - side, cls, 8 + 3 * k + d - 1, place.at(dx=d)).wait_recv()
    for copy in pending:
        copy.wait_send()
    pages.wait()


def row_facts(shape, axis):
    row = lax.broadcasted_iota(jnp.int32, shape, axis)
    inner = row % CLASS_ROWS
    r = row % ROWS
    first = row < CLASS_ROWS
    x = jnp.where(first, inner // ROWS % NX, inner // 32)
    z = jnp.where(first, inner // 16, inner // ROWS % NZ)
    c = jnp.where(first, 0, 1)
    token = (x * 16 + z * 2 + c) * ROWS + r
    return token // SPAN, token % SPAN


def spread_of(values, lane, step, count):
    total = jnp.zeros(lane.shape, jnp.int32)
    for j in range(count):
        total = jnp.where(lane // step == j, values(j), total)
    return total


def new_queries(pieces, lengths, queries):
    apart = lax.broadcasted_iota(jnp.int32, (128, 128), 1) - lax.broadcasted_iota(
        jnp.int32, (128, 128), 0
    )
    source = lax.broadcasted_iota(jnp.int32, (128, 128), 0)

    def block(start, first, columns, width):
        total = None
        for who in range(start // width, (start + 127) // width + 1):
            pick = (apart == who * width - start - first) & (source >= first) & (source < first + width)
            pick = pick.astype(F32).astype(BF16)
            term = jnp.dot(
                pieces[who].reshape(TOKENS, 128), pick, preferred_element_type=F32
            )
            total = term if total is None else total + term
        return total

    request, offset = row_facts((TOKENS, 128), 0)
    lane = lax.broadcasted_iota(jnp.int32, (TOKENS, 128), 1)
    rate = jnp.exp((lane % 64).astype(F32) * (-2.0 / HEAD_SIZE * LOG_BASE))
    position = (jnp.where(request == 0, lengths[0], lengths[1]) + offset).astype(F32)
    angle = position * rate
    cosine = jnp.cos(angle)
    sine = jnp.where(lane < 64, -1.0, 1.0) * jnp.sin(angle)

    def rotate(values):
        return (values * cosine + pltpu.roll(values, 64, 1) * sine).astype(BF16)

    for h in range(QUERY_PER_KV):
        queries[h] = rotate(block(h * HEAD_SIZE, 0, 0, Q_COLS))
    keys = rotate(block(0, Q_COLS, 0, KV_COLS))
    values = block(HEAD_SIZE, Q_COLS, 0, KV_COLS).astype(BF16)
    return jnp.concatenate([keys, values], axis=1)


def split_rows(rows):
    out = []
    for row in rows:
        high = row.astype(BF16).astype(F32)
        middle = (row - high).astype(BF16).astype(F32)
        out += [high, middle, row - high - middle]
    return out


def stack_rows(rows, count):
    at = lax.broadcasted_iota(jnp.int32, (count, TOKENS), 0)
    total = jnp.zeros((count, TOKENS), F32)
    for k, row in enumerate(rows):
        total = jnp.where(at == k, row, total)
    return total


def attend_kernel(
    pieces, landed, cache, lengths, page_table, new_pages_v, new_pages, mig_to, packed, updated,
    queries, joined,
):
    owner = Place().owner()
    new_rows = new_queries(pieces, lengths, queries)

    slot = lax.broadcasted_iota(jnp.int32, (SLOTS, page_table.shape[1]), 0) + owner * SLOTS
    entry_at = lax.broadcasted_iota(jnp.int32, slot.shape, 1) + 1
    new_slot, new_at = slot[:, :REQUEST_PAGES], entry_at[:, :REQUEST_PAGES]

    def found(table, r, ids, at):
        hit = jnp.where(table[r : r + 1, :] == ids, at, 0).astype(F32)
        return jnp.sum(hit, axis=1, keepdims=True)

    facts = [
        found(page_table, 0, slot, entry_at),
        found(page_table, 1, slot, entry_at),
        found(new_pages_v, 0, new_slot, new_at),
        found(new_pages_v, 1, new_slot, new_at),
    ]
    sender = (owner + OWNERS - 1) % OWNERS
    own_slot = lax.broadcasted_iota(jnp.int32, (SLOTS, 1), 0)
    landing = jnp.zeros((SLOTS, 1), F32)
    for j in range(MIGRATED):
        landing = jnp.where(own_slot == mig_to[sender, j], 1.0, landing)
    facts.append(landing)
    lane = lax.broadcasted_iota(jnp.int32, (SLOTS, 128), 1)
    table = jnp.zeros((SLOTS, 128), F32)
    for k, fact in enumerate(facts):
        table = jnp.where(lane == k, fact, table)
    key = lax.broadcasted_iota(jnp.int32, (KEYS, SLOTS), 0)
    belongs = key // PAGE_TOKENS == lax.broadcasted_iota(jnp.int32, (KEYS, SLOTS), 1)
    by_key = jnp.dot(
        belongs.astype(F32).astype(BF16), table.astype(BF16), preferred_element_type=F32
    )
    within = (lax.broadcasted_iota(jnp.int32, (KEYS, 1), 0) % PAGE_TOKENS).astype(F32)

    def least(r):
        old, new = by_key[:, r : r + 1], by_key[:, 2 + r : 3 + r]
        old_ok = (old > 0.5) & ((old - 1.0) * PAGE_TOKENS + within < lengths[r].astype(F32))
        new_first = jnp.where(new > 0.5, (new - 1.0) * PAGE_TOKENS + within, 1e9)
        return jnp.where(old_ok, 0.0, new_first)

    request, offset = row_facts((1, TOKENS), 1)
    needed = jnp.where(request == 0, least(0), least(1))
    bias = jnp.where(offset.astype(F32) >= needed, 0.0, NEG_LARGE)

    total = MIGRATED * PAGE_TOKENS + TOKENS
    lane = lax.broadcasted_iota(jnp.int32, (1, MIGRATED * PAGE_TOKENS), 1)
    migrated_to = (
        spread_of(lambda j: mig_to[sender, j], lane, PAGE_TOKENS, MIGRATED) * PAGE_TOKENS
        + lane % PAGE_TOKENS
    )
    page = request * REQUEST_PAGES + offset // PAGE_TOKENS
    written_to = spread_of(
        lambda j: new_pages[j // REQUEST_PAGES, j % REQUEST_PAGES], page, 1, 2 * REQUEST_PAGES
    )
    written_to = jnp.where(
        written_to // SLOTS == owner, written_to % SLOTS * PAGE_TOKENS + offset % PAGE_TOKENS, -1
    )
    target = jnp.concatenate([migrated_to, written_to], axis=1)
    pick = lax.broadcasted_iota(jnp.int32, (KEYS, total), 0) == target
    arrived = jnp.concatenate(
        [landed[...].reshape(MIGRATED * PAGE_TOKENS, 2 * HEAD_SIZE), new_rows], axis=0
    )
    fresh = jnp.dot(pick.astype(F32).astype(BF16), arrived, preferred_element_type=F32)
    changed = by_key[:, 2:3] + by_key[:, 3:4] + by_key[:, 4:5] > 0.5
    rows = jnp.where(
        changed, fresh, cache[...].reshape(KEYS, 2 * HEAD_SIZE).astype(F32)
    )
    kept = rows.astype(BF16)
    updated[...] = kept.reshape(updated.shape)
    keys = kept[:, :HEAD_SIZE]
    values = rows[:, HEAD_SIZE:].T.astype(BF16)
    tops, sums = [], []
    for h in range(QUERY_PER_KV):
        scores = across(keys, queries[h]) * HEAD_SIZE ** (-0.5) + bias
        top = jnp.max(scores, axis=0, keepdims=True)
        weights = jnp.exp(scores - top)
        tops.append(top)
        sums.append(jnp.sum(weights, axis=0, keepdims=True))
        joined[h * HEAD_SIZE : (h + 1) * HEAD_SIZE, :] = jnp.dot(
            values, weights.astype(BF16), preferred_element_type=F32
        ).astype(BF16)
    for who in range(OWNERS):
        one = who * Q_COLS // HEAD_SIZE
        two = min(one + 1, QUERY_PER_KV - 1)
        packed[who, 0:Q_COLS, :] = joined[who * Q_COLS : (who + 1) * Q_COLS, :]
        packed[who, Q_COLS:, :] = stack_rows(
            split_rows([tops[one], tops[two], sums[one], sums[two]]), PACK - Q_COLS
        ).astype(BF16)


def unpack(ref_value):
    value = ref_value.astype(F32)
    rows = [value[Q_COLS + k : Q_COLS + k + 1] for k in range(12)]
    facts = [rows[3 * k] + rows[3 * k + 1] + rows[3 * k + 2] for k in range(4)]
    return value[:Q_COLS], facts


def merge(parts, who):
    head_end = (who * Q_COLS // HEAD_SIZE + 1) * HEAD_SIZE - who * Q_COLS
    in_first = lax.broadcasted_iota(jnp.int32, (Q_COLS, TOKENS), 0) < head_end
    tops = [parts[0][1][0], parts[0][1][1]]
    for _, facts in parts[1:]:
        tops = [jnp.maximum(tops[k], facts[k]) for k in range(2)]
    total, sums = 0.0, [0.0, 0.0]
    for values, facts in parts:
        scale = [jnp.exp(facts[k] - tops[k]) for k in range(2)]
        sums = [sums[k] + scale[k] * facts[2 + k] for k in range(2)]
        total = total + values * jnp.where(in_first, scale[0], scale[1])
    return total, tops + sums, in_first


def merge_owners(place, packed, near, far, leaving, send, recv):
    side = place.z // 4
    pending = []
    for d in range(1, NX):
        x = (place.x + d) % NX
        copy = remote(
            packed.at[pl.ds(x * 2, 2)], near.at[d - 1], send.at[d], recv.at[d], place.at(dx=d)
        )
        copy.start()
        pending.append(copy)
    for copy in pending:
        copy.wait_recv()

    def gathered(which):
        who = place.x * 2 + which
        parts = [unpack(packed[who])] + [unpack(near[d, which]) for d in range(NX - 1)]
        return merge(parts, who)

    total, facts, _ = gathered(1 - side)
    leaving[0:Q_COLS, :] = total.astype(BF16)
    leaving[Q_COLS:, :] = stack_rows(split_rows(facts), PACK - Q_COLS).astype(BF16)
    copy = remote(leaving, far, send.at[0], recv.at[0], place.at(dz=4))
    copy.start()
    pending.append(copy)
    total, facts, _ = gathered(side)
    copy.wait_recv()
    total, facts, in_first = merge([(total, facts), unpack(far[...])], place.owner())
    for copy in pending:
        copy.wait_send()
    return total / jnp.where(in_first, facts[2], facts[3])


MERGE_SCRATCH = [
    pltpu.VMEM((NX - 1, 2, PACK, TOKENS), BF16),
    pltpu.VMEM((PACK, TOKENS), BF16),
    pltpu.VMEM((PACK, TOKENS), BF16),
    pltpu.SemaphoreType.DMA((NX,)),
    pltpu.SemaphoreType.DMA((NX,)),
]


def exit_kernel(
    packed, stream, gain, out_w, gate_w, up_w, down_w, layer_out,
    out_buf, gate_buf, up_buf, down_buf, hidden, attended, load_sems, *comm
):
    joining, first, gather, second = comm[:5], comm[5:18], comm[18:24], comm[24:]
    place = Place()
    ready = greet(place)
    loads = [
        pltpu.make_async_copy(src, dst, load_sems.at[k])
        for k, (src, dst) in enumerate(
            (
                (out_w, out_buf.at[0:Q_COLS]),
                (gate_w, gate_buf),
                (up_w, up_buf),
                (down_w, down_buf),
            )
        )
    ]
    for load in loads:
        load.start()
    out_buf[Q_COLS:, :] = jnp.zeros((128 - Q_COLS, WIDTH), BF16)
    ready()
    columns = merge_owners(place, packed, *joining)
    columns = jnp.concatenate([columns, jnp.zeros((128 - Q_COLS, TOKENS), F32)], axis=0)
    attended[...] = columns.T.astype(BF16).reshape(attended.shape)
    loads[0].wait()

    def out_term(cls, cols):
        return jnp.dot(attended[cls], out_buf[:, cols], preferred_element_type=F32)

    summed = scatter_sums(place, out_term, first)
    mixed = (stream[...].astype(F32) + summed).astype(BF16)
    block = rms_block(mixed.astype(F32), gain)
    gather_rows(place, block, gather)
    loads[1].wait()
    loads[2].wait()

    def hide(cls):
        rows = gather[2][cls]
        gate = jnp.dot(rows, gate_buf[...], preferred_element_type=F32)
        up = jnp.dot(rows, up_buf[...], preferred_element_type=F32)
        hidden[cls] = (gate / (1.0 + jnp.exp(-gate)) * up).astype(BF16)

    hide(place.c)
    gather_pair_wait(place, gather)
    hide(1 - place.c)
    loads[3].wait()

    def down_term(cls, cols):
        return jnp.dot(hidden[cls], down_buf[:, cols], preferred_element_type=F32)

    summed = scatter_sums(place, down_term, second)
    layer_out[...] = (mixed.astype(F32) + summed).astype(BF16)


VM = pl.BlockSpec(memory_space=pltpu.VMEM)
SM = pl.BlockSpec(memory_space=pltpu.SMEM)
ANY = pl.BlockSpec(memory_space=pl.ANY)
VMEM_BYTES = 60 * 2**20


def entry(stream, gain, query_w, kv_w, query_b, kv_b, cache, mig_from):
    page = (PAGE_TOKENS, 2 * HEAD_SIZE)
    return pl.pallas_call(
        entry_kernel,
        out_shape=(
            jax.ShapeDtypeStruct((OWNERS, 2, CLASS_ROWS, 128), BF16),
            jax.ShapeDtypeStruct((MIGRATED,) + page, BF16),
        ),
        in_specs=[VM, VM, ANY, ANY, VM, VM, ANY, SM],
        out_specs=(VM, VM),
        scratch_shapes=[
            pltpu.VMEM((128, WIDTH), BF16),
            pltpu.VMEM((SLOTS,) + page, BF16),
            pltpu.VMEM((MIGRATED,) + page, BF16),
            pltpu.SemaphoreType.DMA((3,)),
            pltpu.SemaphoreType.DMA((2,)),
            pltpu.SemaphoreType.DMA((14,)),
            pltpu.SemaphoreType.DMA((14,)),
        ]
        + GATHER_SCRATCH,
        compiler_params=pltpu.CompilerParams(
            collective_id=0, has_side_effects=True, vmem_limit_bytes=VMEM_BYTES
        ),
        name="entry",
    )(stream, gain, query_w, kv_w, query_b, kv_b, cache, mig_from)


def attend(pieces, landed, cache, lengths, page_table, new_pages, mig_to):
    return pl.pallas_call(
        attend_kernel,
        out_shape=(
            jax.ShapeDtypeStruct((OWNERS, PACK, TOKENS), BF16),
            jax.ShapeDtypeStruct((1,) + cache.shape, BF16),
        ),
        in_specs=[VM, VM, VM, SM, VM, VM, SM, SM],
        out_specs=(VM, VM),
        scratch_shapes=[
            pltpu.VMEM((QUERY_PER_KV, TOKENS, HEAD_SIZE), BF16),
            pltpu.VMEM((QUERY_PER_KV * HEAD_SIZE, TOKENS), BF16),
        ],
        compiler_params=pltpu.CompilerParams(vmem_limit_bytes=VMEM_BYTES),
        name="attend",
    )(pieces, landed, cache, lengths, page_table, new_pages, new_pages, mig_to)


def leave(packed, stream, gain, out_w, gate_w, up_w, down_w):
    buffers = [
        pltpu.VMEM(shape, BF16)
        for shape in ((128, WIDTH), gate_w.shape, up_w.shape, down_w.shape)
    ]
    return pl.pallas_call(
        exit_kernel,
        out_shape=jax.ShapeDtypeStruct((ROWS, WIDTH), BF16),
        in_specs=[VM, VM, VM, ANY, ANY, ANY, ANY],
        out_specs=VM,
        scratch_shapes=buffers
        + [
            pltpu.VMEM((2, CLASS_ROWS, gate_w.shape[1]), BF16),
            pltpu.VMEM((2, CLASS_ROWS, 128), BF16),
            pltpu.SemaphoreType.DMA((4,)),
        ]
        + MERGE_SCRATCH
        + SCATTER_SCRATCH
        + GATHER_SCRATCH
        + SCATTER_SCRATCH,
        compiler_params=pltpu.CompilerParams(
            collective_id=1, has_side_effects=True, vmem_limit_bytes=VMEM_BYTES
        ),
        name="leave",
    )(packed, stream, gain, out_w, gate_w, up_w, down_w)


def per_device(
    stream,
    attn_gain,
    query_weight,
    query_bias_input,
    key_value_weight,
    key_value_bias,
    output_weight,
    mlp_gain,
    w_gate,
    w_up,
    w_down,
    paged_cache_input,
    lengths,
    page_table,
    new_pages,
    mig_from,
    mig_to,
):
    lines = (WIDTH // 128, 128)
    cache = paged_cache_input[0]
    pieces, landed = entry(
        stream,
        attn_gain.reshape(lines),
        query_weight[:, 0, :].T,
        key_value_weight[:, 0, :].T,
        query_bias_input,
        key_value_bias,
        cache,
        mig_from,
    )
    packed, updated_cache = attend(pieces, landed, cache, lengths, page_table, new_pages, mig_to)
    layer_out = leave(
        packed, stream, mlp_gain.reshape(lines), output_weight[0], w_gate, w_up, w_down
    )
    return (layer_out, updated_cache)


def solution(mesh):
    placed = (
        P(("rep", "tp"), None),
        P(),
        P(None, "tp", None),
        P("tp", None),
        P(None, "tp", None),
        P("tp", None),
        P("tp", None, None),
        P(),
        P(None, "tp"),
        P(None, "tp"),
        P("tp", None),
        P(("rep", "tp"), None, None, None),
        P("rep"),
        P("rep", None),
        P("rep", None),
        P("rep", None),
        P("rep", None),
    )
    return jax.shard_map(
        per_device,
        mesh=mesh,
        in_specs=placed,
        out_specs=(P(("rep", "tp"), None), P(("rep", "tp"), None, None, None)),
        check_vma=False,
    )
```

time: 232 us -> 149 us (0.64)
  waiting for transfers between devices: 43.8 us -> 0 us
  starting transfers between devices: 27.9 us -> 0 us
  Pallas kernels: 127 us -> 146 us
  local copies, waits for them, and re-layouts: 17.7 us -> 1.41 us
  other arithmetic: 11.9 us -> 0 us
  matrix products: 2.38 us -> 0 us
    ppermute x13 -> x0, waiting for transfers between devices: 43.8 us -> none  [the longest x12 43.8 us: from_partner(): return lax.ppermute(value, axis, pairs)]
    ppermute x13 -> x0, starting transfers between devices: 27.9 us -> none  [the longest x12 20.7 us: from_partner(): return lax.ppermute(value, axis, pairs)]
    pallas_call x1 -> x2, Pallas kernels: 27 us -> 51.8 us  [the longest x1 44.4 us: entry(): pl.pallas_call(entry_kernel, out_shape=(jax.ShapeDtypeStruct((OWNERS, 2,...]
    unnamed x17 -> x1, local copies, waits for them, and re-layouts: 6.96 us -> 1.41 us
    gather x3 -> x0, local copies, waits for them, and re-layouts: 5.07 us -> none  [the longest x1 3.94 us: per_device(): fresh_pages = appended_rows[row_of_token(source_rows)]]
    pallas_call x1, Pallas kernels: 99.5 us -> 94.5 us  [leave(): pl.pallas_call(exit_kernel, out_shape=jax.ShapeDtypeStruct((ROWS, WIDTH),...]
    select_n x10 -> x0, other arithmetic: 3.21 us -> none  [the longest x1 1.3 us: key_allowed(): old_limit = jnp.repeat(jnp.take(lengths, old_prompt), PAGE_TOKENS)]
    dot_general x2 -> x0, matrix products: 2.38 us -> none  [the longest x1 1.24 us: per_device(): jnp.einsum('qtk,kd->tqd', prob_bf, flat_keys[:, HEAD_SIZE:], preferred_el...]
  transfers between devices with their start and end apart: 13 -> 0, of which waited for: 8 -> 0; matrix products, arithmetic and copies ran while one was open for 8% -> 0% of each run, Pallas kernels for 12% -> 0%
where the time goes in v2:
time: 149 us; the launch traced here: 148 us
  Pallas kernels  146 us (98%)
    pallas_call x1, Pallas kernels, leave(): pl.pallas_call(exit_kernel, out_shape=jax.ShapeDtypeStruct((ROWS, WIDTH),...  94.5 us
    pallas_call x1, Pallas kernels, entry(): pl.pallas_call(entry_kernel, out_shape=(jax.ShapeDtypeStruct((OWNERS, 2,...  44.4 us
    pallas_call x1, Pallas kernels, attend(): pl.pallas_call(attend_kernel, out_shape=(jax.ShapeDtypeStruct((OWNERS, PA...  7.34 us

profile of v2, /device:TPU:16, one launch (start us, length us, event | category | flops | bytes accessed | tf_op | source)
XLA Modules:
  0.0 148.4 jit_solution(8908670971355203171)
XLA Ops:
  0.6 44.4 %entry.1 = (bf16[8,2,128,128]{3,2,1,0:T(8,128)(2,1)}, bf16[8,16,256]{2,1,0:T(8,128)(2,1)}) custom-call(bf16[4,5120]{1,0:T(4,128)(2,1)} %stream.3, bf16[40,128]{1,0:T(8,128)(2,1)} %bitcast.15, bf16[80,5120]{1,0:T(8,128)(2,1)} %bitcast.13, bf16[32,5120]{1,0:T(8,128)(2,1)} %bitcast.14, bf16[1,80]{1,0:T(2,128)(2,1)} %query_b.1, bf16[1,32]{1,0:T(2,128)(2,1)} %kv_b.1, ...), custom_call_target="tpu_custom_call" | custom-call | tf_op jit(solution)/shard_map/entry/pallas_call | solution.py:678
  45.1 7.3 %attend.1 = (bf16[8,96,256]{2,1,0:T(8,128)(2,1)}, bf16[1,64,16,256]{3,2,1,0:T(8,128)(2,1)}) custom-call(bf16[8,2,128,128]{3,2,1,0:T(8,128)(2,1)} %get-tuple-element.6.pieces, bf16[8,16,256]{2,1,0:T(8,128)(2,1)} %get-tuple-element.7.landed, bf16[64,16,256]{2,1,0:T(8,128)(2,1)} %bitcast.11, s32[2]{0:T(128)} %lengths.1, s32[2,192]{1,0:T(2,128)} %page_table.1, ...), custom_call_target="tpu_custom_call" | custom-call | tf_op jit(solution)/shard_map/attend/pallas_call | solution.py:704
  52.4 94.5 %leave.1 = bf16[4,5120]{1,0:T(4,128)(2,1)} custom-call(bf16[8,96,256]{2,1,0:T(8,128)(2,1)} %get-tuple-element.8.packed, bf16[4,5120]{1,0:T(4,128)(2,1)} %stream.3, bf16[40,128]{1,0:T(8,128)(2,1)} %bitcast.16, bf16[80,5120]{1,0:T(8,128)(2,1)} %bitcast.12, bf16[5120,256]{1,0:T(8,128)(2,1)} %gate_w.1, bf16[5120,256]{1,0:T(8,128)(2,1)} %up_w.1, ...), custom_call_target="tpu_custom_call" | custom-call | tf_op jit(solution)/shard_map/leave/pallas_call | solution.py:726
  147.0 1.4 copy.20

commit v3 on v2

--- a/solution.py
+++ b/solution.py
@@ -24,7 +24,9 @@
 ROWS = 4
 CLASS_ROWS = 128
 WIDTH = 5120
-HALF = WIDTH // 2
+PARTS = 4
+PART = WIDTH // PARTS
+SEMS = 8 * PARTS + 16
 MESH = pl.DeviceIdType.MESH
 BF16, F32 = jnp.bfloat16, jnp.float32
 
@@ -79,16 +81,20 @@
     return pl.ds(pl.multiple_of(index * size, size), size)
 
 
-def cols_at(half):
-    return pl.ds(half * HALF, HALF)
+def cols_at(part):
+    return pl.ds(pl.multiple_of(part * PART, PART), PART)
+
+
+def part_of(k, side):
+    return (k + side * PARTS // 2) % PARTS
 
 
 GATHER_SCRATCH = [
     pltpu.VMEM((NZ, ROWS, WIDTH), BF16),
     pltpu.VMEM((32, WIDTH), F32),
     pltpu.VMEM((2, CLASS_ROWS, WIDTH), BF16),
-    pltpu.SemaphoreType.DMA((24,)),
-    pltpu.SemaphoreType.DMA((24,)),
+    pltpu.SemaphoreType.DMA((SEMS,)),
+    pltpu.SemaphoreType.DMA((SEMS,)),
     pltpu.SemaphoreType.DMA((2,)),
 ]
 
@@ -120,34 +126,37 @@
 
     partner = place.at(flip=True)
 
-    def to_partner(owner, half):
-        part = gathered.at[cls, rows_at(owner, height), cols_at(half)]
-        remote(part, part, pair.at[0], pair.at[1], partner).start()
+    def to_partner(ref):
+        remote(ref, ref, pair.at[0], pair.at[1], partner).start()
 
     steps = n2 // 2
+
+    def tile_at(side, s, k):
+        owner = (i2 - (1 - 2 * side) * s + n2) % n2
+        return gathered.at[cls, rows_at(owner, height), cols_at(part_of(k, side))]
+
+    def hop(ref, side, s, k):
+        slot = 7 + (side * steps + s) * PARTS + k
+        return remote(ref, ref, send.at[slot], recv.at[slot], shift(second, 1 - 2 * side))
+
+    def landed(side, s, k):
+        ref = tile_at(side, s, k)
+        hop(ref, side, s - 1, k).wait_recv()
+        return ref
+
     for s in range(steps):
-        for half in range(2):
-            for side, sign in ((0, 1), (1, -1)):
-                owner = (i2 - sign * s + n2) % n2
-                part = gathered.at[cls, rows_at(owner, height), cols_at(half)]
-                slot = 7 + side * 8 + s * 2 + half
-                if s >= 1:
-                    before = slot - 2
-                    remote(
-                        part, part, send.at[before], recv.at[before], shift(second, sign)
-                    ).wait_recv()
-                if s < steps - 1 or half == side:
-                    copy = remote(part, part, send.at[slot], recv.at[slot], shift(second, sign))
+        for k in range(PARTS):
+            for side in range(2):
+                ref = landed(side, s, k) if s >= 1 else tile_at(side, s, k)
+                if s < steps - 1 or k < PARTS // 2:
+                    copy = hop(ref, side, s, k)
                     copy.start()
                     pending.append(copy)
                 if s >= 1 or side == 0:
-                    to_partner(owner, half)
-    far = (i2 + steps) % n2
-    for side, sign in ((0, 1), (1, -1)):
-        part = gathered.at[cls, rows_at(far, height), cols_at(side)]
-        slot = 7 + side * 8 + (steps - 1) * 2 + side
-        remote(part, part, send.at[slot], recv.at[slot], shift(second, sign)).wait_recv()
-        to_partner(far, side)
+                    to_partner(ref)
+    for k in range(PARTS // 2):
+        for side in range(2):
+            to_partner(landed(side, steps, k))
     for copy in pending:
         copy.wait_send()
 
@@ -175,23 +184,39 @@
     pltpu.VMEM((CLASS_ROWS, WIDTH), BF16),
     pltpu.VMEM((CLASS_ROWS, WIDTH), BF16),
     pltpu.VMEM((CLASS_ROWS, WIDTH), F32),
-    pltpu.VMEM((8, 32, HALF), BF16),
-    pltpu.VMEM((8, 32, HALF), BF16),
+    pltpu.VMEM((4 * PARTS, 32, PART), BF16),
+    pltpu.VMEM((4 * PARTS, 32, PART), BF16),
     pltpu.VMEM((32, WIDTH), F32),
     pltpu.VMEM((NZ, ROWS, WIDTH), BF16),
     pltpu.VMEM((NZ, ROWS, WIDTH), BF16),
     pltpu.VMEM((NZ, ROWS, WIDTH), F32),
     pltpu.VMEM((ROWS, WIDTH), F32),
-    pltpu.SemaphoreType.DMA((24,)),
-    pltpu.SemaphoreType.DMA((24,)),
-    pltpu.SemaphoreType.DMA((2,)),
+    pltpu.SemaphoreType.DMA((SEMS,)),
+    pltpu.SemaphoreType.DMA((SEMS,)),
+    pltpu.SemaphoreType.DMA((2 * PARTS,)),
 ]
+
+
+def swap_of(place, scratch):
+    handed, swapped, pair = scratch[0], scratch[1], scratch[12]
+
+    def swap(part):
+        return remote(
+            handed.at[:, cols_at(part)],
+            swapped.at[:, cols_at(part)],
+            pair.at[part],
+            pair.at[PARTS + part],
+            place.at(flip=True),
+        )
+
+    return swap
 
 
 def scatter_class(place, scratch, along):
     _, swapped, own, outgoing, incoming, tile, leaving, arriving, parts, result, send, recv, _ = (
         scratch
     )
+    swap = swap_of(place, scratch)
     n1, n2 = (NZ, NX) if along == "z" else (NX, NZ)
     i1, i2 = (place.z, place.x) if along == "z" else (place.x, place.z)
     first, second = ("z", "x") if along == "z" else ("x", "z")
@@ -205,8 +230,8 @@
             return ref.at[slot]
         return ref.at[slot // 2, pl.ds((slot % 2) * 16, 16)]
 
-    def mine(owner, half):
-        rows, cols = rows_at(owner, height), cols_at(half)
+    def mine(owner, part):
+        rows, cols = rows_at(owner, height), cols_at(part)
         return own[rows, cols] + swapped[rows, cols].astype(F32)
 
     steps = n1 // 2
@@ -221,29 +246,33 @@
             shift(first, sign),
         )
 
+    def slot_at(side, s, k):
+        return (side * steps + s) * PARTS + k
+
+    early, late = list(range(PARTS // 2)), list(range(PARTS // 2, PARTS))
     for s in range(steps):
-        for half in range(2):
+        for k in early if s == 0 else late + early:
             for side, sign in ((0, 1), (1, -1)):
-                begin = 0 if half == side else 1
-                if s < begin:
-                    continue
+                part = part_of(k, side)
+                if s == 0:
+                    swap(part).wait_recv()
                 owner = (i1 + sign * (steps - s) + 2 * n1) % n1
-                slot = side * steps * 2 + s * 2 + half
-                value = mine(owner, half)
-                if s > begin:
-                    hop(slot - 2, sign).wait_recv()
-                    value = value + slot_of(incoming, slot - 2)[...].astype(F32)
+                slot = slot_at(side, s, k)
+                value = mine(owner, part)
+                if s > (0 if k in early else 1):
+                    hop(slot - PARTS, sign).wait_recv()
+                    value = value + slot_of(incoming, slot - PARTS)[...].astype(F32)
                 slot_of(outgoing, slot)[...] = value.astype(BF16)
                 copy = hop(slot, sign)
                 copy.start()
                 pending.append(copy)
-    for half in range(2):
-        value = mine(i1, half)
+    for part in range(PARTS):
+        value = mine(i1, part)
         for side, sign in ((0, 1), (1, -1)):
-            slot = side * steps * 2 + (steps - 1) * 2 + half
+            slot = slot_at(side, steps - 1, part_of(part, side))
             hop(slot, sign).wait_recv()
             value = value + slot_of(incoming, slot)[...].astype(F32)
-        tile[0:height, cols_at(half)] = value
+        tile[0:height, cols_at(part)] = value
 
     for j in range(n2):
         part = tile[j * ROWS : (j + 1) * ROWS, :]
@@ -254,8 +283,8 @@
         return remote(
             leaving.at[(i2 + d) % n2],
             arriving.at[d],
-            send.at[16 + d],
-            recv.at[16 + d],
+            send.at[8 * PARTS + d],
+            recv.at[8 * PARTS + d],
             shift(second, d),
         )
 
@@ -273,25 +302,23 @@
 
 
 def scatter_sums(place, partial, scratch):
-    handed, swapped, own = scratch[:3]
-    pair = scratch[12]
+    handed, own = scratch[0], scratch[2]
+    swap = swap_of(place, scratch)
     other = 1 - place.c
-    chunk = 1280
-
-    @pl.loop(0, WIDTH // chunk)
+
+    @pl.loop(0, PARTS // 2)
     def _(k):
-        cols = pl.ds(pl.multiple_of(k * chunk, chunk), chunk)
-        handed[:, cols] = partial(other, cols).astype(BF16)
-        remote(
-            handed.at[:, cols], swapped.at[:, cols], pair.at[0], pair.at[1], place.at(flip=True)
-        ).start()
-
-    @pl.loop(0, WIDTH // chunk)
+        for side in range(2):
+            part = k + side * (PARTS // 2)
+            cols = cols_at(part)
+            handed[:, cols] = partial(other, cols).astype(BF16)
+            swap(part).start()
+
+    @pl.loop(0, PARTS // 2)
     def _(k):
-        cols = pl.ds(pl.multiple_of(k * chunk, chunk), chunk)
-        own[:, cols] = partial(place.c, cols)
-
-    remote(handed, swapped, pair.at[0], pair.at[1], place.at(flip=True)).wait()
+        for side in range(2):
+            cols = cols_at(k + side * (PARTS // 2))
+            own[:, cols] = partial(place.c, cols)
 
     @pl.when(place.c == 0)
     def _():
@@ -301,6 +328,8 @@
     def _():
         scatter_class(place, scratch, "x")
 
+    for part in range(PARTS):
+        swap(part).wait_send()
     return scratch[9][...]
 
 

time: 149 us -> 138 us (0.926)
  Pallas kernels: 146 us -> 136 us
    pallas_call x1, Pallas kernels: 94.5 us -> 86.6 us  [leave(): pl.pallas_call(exit_kernel, out_shape=jax.ShapeDtypeStruct((ROWS, WIDTH),...]
    pallas_call x1, Pallas kernels: 44.4 us -> 42.1 us  [entry(): pl.pallas_call(entry_kernel, out_shape=(jax.ShapeDtypeStruct((OWNERS, 2,...]
where the time goes in v3:
time: 138 us
  Pallas kernels  136 us (99%)
  local copies, waits for them, and re-layouts  1.41 us (1%)
    pallas_call x1, Pallas kernels, leave(): pl.pallas_call(exit_kernel, out_shape=jax.ShapeDtypeStruct((ROWS, WIDTH),...  86.6 us
    pallas_call x1, Pallas kernels, entry(): pl.pallas_call(entry_kernel, out_shape=(jax.ShapeDtypeStruct((OWNERS, 2,...  42.1 us
    pallas_call x1, Pallas kernels, attend(): pl.pallas_call(attend_kernel, out_shape=(jax.ShapeDtypeStruct((OWNERS, PA...  7.34 us

profile of v3, /device:TPU:16, one launch (start us, length us, event | category | flops | bytes accessed | tf_op | source)
XLA Modules:
  0.0 138.1 jit_solution(5570604087574618404)
XLA Ops:
  0.6 42.1 %entry.1 = (bf16[8,2,128,128]{3,2,1,0:T(8,128)(2,1)}, bf16[8,16,256]{2,1,0:T(8,128)(2,1)}) custom-call(bf16[4,5120]{1,0:T(4,128)(2,1)} %stream.3, bf16[40,128]{1,0:T(8,128)(2,1)} %bitcast.15, bf16[80,5120]{1,0:T(8,128)(2,1)} %bitcast.13, bf16[32,5120]{1,0:T(8,128)(2,1)} %bitcast.14, bf16[1,80]{1,0:T(2,128)(2,1)} %query_b.1, bf16[1,32]{1,0:T(2,128)(2,1)} %kv_b.1, ...), custom_call_target="tpu_custom_call" | custom-call | tf_op jit(solution)/shard_map/entry/pallas_call | solution.py:707
  42.8 7.3 %attend.1 = (bf16[8,96,256]{2,1,0:T(8,128)(2,1)}, bf16[1,64,16,256]{3,2,1,0:T(8,128)(2,1)}) custom-call(bf16[8,2,128,128]{3,2,1,0:T(8,128)(2,1)} %get-tuple-element.6.pieces, bf16[8,16,256]{2,1,0:T(8,128)(2,1)} %get-tuple-element.7.landed, bf16[64,16,256]{2,1,0:T(8,128)(2,1)} %bitcast.11, s32[2]{0:T(128)} %lengths.1, s32[2,192]{1,0:T(2,128)} %page_table.1, ...), custom_call_target="tpu_custom_call" | custom-call | tf_op jit(solution)/shard_map/attend/pallas_call | solution.py:733
  50.1 86.6 %leave.1 = bf16[4,5120]{1,0:T(4,128)(2,1)} custom-call(bf16[8,96,256]{2,1,0:T(8,128)(2,1)} %get-tuple-element.8.packed, bf16[4,5120]{1,0:T(4,128)(2,1)} %stream.3, bf16[40,128]{1,0:T(8,128)(2,1)} %bitcast.16, bf16[80,5120]{1,0:T(8,128)(2,1)} %bitcast.12, bf16[5120,256]{1,0:T(8,128)(2,1)} %gate_w.1, bf16[5120,256]{1,0:T(8,128)(2,1)} %up_w.1, ...), custom_call_target="tpu_custom_call" | custom-call | tf_op jit(solution)/shard_map/leave/pallas_call | solution.py:755
  136.7 1.4 %copy.20 = bf16[4,5120]{1,0:T(4,128)(2,1)} copy(bf16[4,5120]{1,0:T(4,128)(2,1)} %leave.1) | data formatting | bytes 81920
